TPU v7x, 32 devices: a whole 2x2x4 slice. The times are simulated.
32 devices in a mesh: ctx: 8 (over y, x, core), fsdp: 4 (over z).
Axes of the slice: x: 2, y: 2, z: 4, core: 2. Of those that a mesh axis runs over, the one named last changes fastest.
Arguments:
- tokens: bfloat16 [4, 1024, 1024], P('fsdp', 'ctx'), may hold values from -6 to 6
- first_gain: bfloat16 [1024], P('fsdp'), may hold values from 0.5 to 1.5
- query_weight: bfloat16 [1024, 1024], P('fsdp'), may hold values from -0.1875 to 0.1875
- key_weight: bfloat16 [1024, 512], P('fsdp'), may hold values from -0.1875 to 0.1875
- value_weight: bfloat16 [1024, 512], P('fsdp'), may hold values from -0.1875 to 0.1875
- output_weight: bfloat16 [1024, 1024], P('fsdp'), may hold values from -4 to 4
- second_gain: bfloat16 [1024], P('fsdp'), may hold values from 0.5 to 1.5
- router_weight: bfloat16 [1024, 16], P('fsdp'), may hold values from -0.25 to 0.25
- expert_in: bfloat16 [1024, 16, 1024], P('fsdp', 'ctx'), may hold values from -0.1875 to 0.1875
- expert_out: bfloat16 [1024, 16, 512], P('fsdp', 'ctx'), may hold values from -1.796875 to 1.796875
- chosen: int32 [4, 1024, 8], P('fsdp', 'ctx'), may hold values from 0 to 15, all different within a row; in each aligned block of 128 rows (0 to 127, 128 to 255, ..., all dimensions but the last counted through in order) at most 64 rows name the same one
- out_grad: bfloat16 [4, 1024, 1024], P('fsdp', 'ctx'), may hold values from -6 to 6
Outputs:
- layer_out: bfloat16 [4, 1024, 1024], P('fsdp', 'ctx')
- tokens_grad: float32 [4, 1024, 1024], P('fsdp', 'ctx')
- first_gain_grad: float32 [1024], P('fsdp')
- query_grad: float32 [1024, 1024], P('fsdp')
- key_grad: float32 [1024, 512], P('fsdp')
- value_grad: float32 [1024, 512], P('fsdp')
- output_weight_grad: float32 [1024, 1024], P('fsdp')
- second_gain_grad: float32 [1024], P('fsdp')
- router_grad: float32 [1024, 16], P('fsdp')
- expert_in_grad: float32 [1024, 16, 1024], P('fsdp', 'ctx')
- expert_out_grad: float32 [1024, 16, 512], P('fsdp', 'ctx')
Inputs may be any that keep to these rules, and one draw needn't show every extreme that they name: `chosen`: each token names 8 different experts. In each aligned block of 128 positions of a sequence (the positions on one device) no expert is named by more than 64 tokens, a bound that some block reaches.
All inputs are finite; a program needn't handle non-finite values.
Results may differ from a plain program's by a relative error of at most 0.025.
Values may be sent and summed in bfloat16 or wider, within the bound.
No kernel may reach another device: no remote copies, remote signals or barrier semaphores. Data moves between devices by JAX's collectives and lax.ppermute only.
A program may use at most 192 MiB of HBM per device.

v0:
```python
import jax
import jax.numpy as jnp
from jax import lax
from jax.sharding import PartitionSpec as P

HEADS = 16
KV_HEADS = 8
HEAD_DIM = 64
FF = 512
MOST = 64


EPSILON = 1e-06
RESIDUAL = 0.22
ROPE_BASE = 10000.0
HIGHEST = lax.Precision.HIGHEST


def rms_gain(values, gain_vec):
    scales = lax.rsqrt(jnp.mean(values * values, axis=-1, keepdims=True) + EPSILON)
    return (values * scales * gain_vec, scales)


def norm_back(values, scales, gain_vec, upstream):
    weighted = upstream * gain_vec
    gain_term = jnp.sum(upstream * values * scales, axis=(0, 1))
    inner_mean = jnp.mean(weighted * values, axis=-1, keepdims=True)
    return (scales * weighted - values * scales * scales * scales * inner_mean, gain_term)


def rotate(values, positions, direction):
    middle = values.shape[-1] // 2
    inverse = ROPE_BASE ** (-jnp.arange(middle, dtype=jnp.float32) / middle)
    angles = positions.astype(jnp.float32)[:, None] * inverse[None, :]
    cosine = jnp.cos(angles)[:, None, :]
    sine_table = direction * jnp.sin(angles)[:, None, :]
    front_half = values[..., :middle]
    back_half = values[..., middle:]
    return jnp.concatenate(
        [
            front_half * cosine - back_half * sine_table,
            back_half * cosine + front_half * sine_table,
        ],
        axis=-1,
    )


def per_device(
    tokens,
    first_gain,
    query_weight,
    key_weight,
    value_weight,
    output_weight,
    second_gain,
    router_weight,
    expert_in,
    expert_out,
    chosen,
    out_grad,
):
    gain_one, w_query, w_key, w_value, w_output, gain_two, w_router, w_gate_up, w_down = (
        lax.all_gather(first_gain, "fsdp", axis=0, tiled=True),
        lax.all_gather(query_weight, "fsdp", axis=0, tiled=True),
        lax.all_gather(key_weight, "fsdp", axis=0, tiled=True),
        lax.all_gather(value_weight, "fsdp", axis=0, tiled=True),
        lax.all_gather(output_weight, "fsdp", axis=0, tiled=True),
        lax.all_gather(second_gain, "fsdp", axis=0, tiled=True),
        lax.all_gather(router_weight, "fsdp", axis=0, tiled=True),
        lax.all_gather(expert_in, "fsdp", axis=0, tiled=True),
        lax.all_gather(expert_out, "fsdp", axis=0, tiled=True),
    )
    seq_count, ctx_len, width = tokens.shape
    group_size = HEADS // KV_HEADS
    ctx_size = lax.axis_size("ctx")
    ctx_place = lax.axis_index("ctx")
    positions = ctx_place * ctx_len + jnp.arange(ctx_len, dtype=jnp.int32)
    last_pos = ctx_place * ctx_len + ctx_len - 1
    inputs = tokens.astype(jnp.float32)
    gain_first = gain_one.astype(jnp.float32)
    normed_one, scale_one = rms_gain(inputs, gain_first)
    first_low = normed_one.astype(jnp.bfloat16)
    query_proj = jnp.einsum("sqd,de->sqe", first_low, w_query, preferred_element_type=jnp.float32)
    key_proj = jnp.einsum("sqd,de->sqe", first_low, w_key, preferred_element_type=jnp.float32)
    value_proj = jnp.einsum("sqd,de->sqe", first_low, w_value, preferred_element_type=jnp.float32)
    queries = rotate(
        query_proj.reshape(seq_count, ctx_len, HEADS, HEAD_DIM), positions, 1.0
    ).astype(jnp.bfloat16)
    grouped = queries.reshape(seq_count, ctx_len, KV_HEADS, group_size, HEAD_DIM)
    keys = (
        rotate(key_proj.reshape(seq_count, ctx_len, KV_HEADS, HEAD_DIM), positions, 1.0)
        .astype(jnp.bfloat16)
        .reshape(seq_count, ctx_len, KV_HEADS * HEAD_DIM)
    )
    values = value_proj.astype(jnp.bfloat16)
    start_max = jnp.full((seq_count, KV_HEADS, group_size, ctx_len), -1e30, jnp.float32)
    start_sum = jnp.zeros((seq_count, KV_HEADS, group_size, ctx_len), jnp.float32)
    start_acc = jnp.zeros((seq_count, KV_HEADS, group_size, ctx_len, HEAD_DIM), jnp.float32)
    shard_piece = (
        lax.all_gather(keys, "ctx", axis=1, tiled=True),
        lax.all_gather(values, "ctx", axis=1, tiled=True),
    )

    def attend_compute(carried):
        run_max, run_sum, run_acc = carried
        key_piece, value_piece = shard_piece
        key_count = key_piece.shape[1]
        key_heads = key_piece.reshape(seq_count, key_count, KV_HEADS, HEAD_DIM)
        value_heads = value_piece.reshape(seq_count, key_count, KV_HEADS, HEAD_DIM)
        scores = (
            jnp.einsum("sqgrd,skgd->sgrqk", grouped, key_heads, preferred_element_type=jnp.float32)
            * 0.125
        )
        allowed = jnp.arange(key_count, dtype=jnp.int32)[None, :] <= positions[:, None]
        scores = jnp.where(allowed, scores, -jnp.inf)
        new_max = jnp.maximum(run_max, jnp.max(scores, axis=-1))
        weights = jnp.exp(scores - new_max[..., None])
        new_sum = jnp.sum(weights, axis=-1)
        update = jnp.einsum(
            "sgrqk,skgd->sgrqd",
            weights.astype(jnp.bfloat16),
            value_heads,
            preferred_element_type=jnp.float32,
        )
        return (new_max, new_sum, update)

    def unchanged(carried):
        return carried

    run_max, run_sum, run_acc = lax.cond(
        jnp.int32(0) <= last_pos, attend_compute, unchanged, (start_max, start_sum, start_acc)
    )
    attn_heads = run_acc / run_sum[..., None]
    log_total = run_max + jnp.log(run_sum)
    attended = jnp.transpose(attn_heads, (0, 3, 1, 2, 4)).reshape(
        seq_count, ctx_len, HEADS * HEAD_DIM
    )
    attended_low = attended.astype(jnp.bfloat16)
    branch = jnp.einsum("sqe,ed->sqd", attended_low, w_output, preferred_element_type=jnp.float32)
    hidden = inputs + RESIDUAL * branch
    gain_second = gain_two.astype(jnp.float32)
    second_normalized, scale_two = rms_gain(hidden, gain_second)
    second_low = second_normalized.astype(jnp.bfloat16)
    logits = jnp.einsum("sqd,de->sqe", second_low, w_router, preferred_element_type=jnp.float32)
    expert_count = w_router.shape[1]
    picked = jnp.sum(
        (chosen[..., None] == jnp.arange(expert_count, dtype=jnp.int32)).astype(jnp.float32), axis=2
    )
    gate_probs = jax.nn.softmax(jnp.where(picked > 0, logits, -1e30), axis=-1) * picked
    slot_rank = jnp.cumsum(picked, axis=1) - picked
    picker = (
        jnp.swapaxes(slot_rank, 1, 2)[:, :, None, :] == jnp.arange(MOST, dtype=jnp.float32)[:, None]
    ).astype(jnp.float32) * jnp.swapaxes(picked, 1, 2)[:, :, None, :]
    picker_low = picker.astype(jnp.bfloat16)
    outgoing = jnp.einsum(
        "sejq,sqd->sejd", picker_low, second_low, preferred_element_type=jnp.float32
    ).astype(jnp.bfloat16)
    gate_slot = jnp.einsum("sejq,sqe->sej", picker, gate_probs, precision=HIGHEST)
    received = lax.all_to_all(outgoing, "ctx", split_axis=1, concat_axis=2, tiled=True)
    gate_up = jnp.einsum("serd,def->serf", received, w_gate_up, preferred_element_type=jnp.float32)
    active = (jax.nn.silu(gate_up[..., :FF]) * gate_up[..., FF:]).astype(jnp.bfloat16)
    result = jnp.einsum(
        "serf,def->serd", active, w_down, preferred_element_type=jnp.float32
    ).astype(jnp.bfloat16)
    returned = lax.all_to_all(result, "ctx", split_axis=2, concat_axis=1, tiled=True)
    returned_f = returned.astype(jnp.float32)
    weighted_rows = returned_f * gate_slot[..., None]
    weighted_high = weighted_rows.astype(jnp.bfloat16)
    weighted_rest = (weighted_rows - weighted_high.astype(jnp.float32)).astype(jnp.bfloat16)
    mixture = jnp.einsum(
        "sejq,sejd->sqd", picker_low, weighted_high, preferred_element_type=jnp.float32
    )
    mixture = mixture + jnp.einsum(
        "sejq,sejd->sqd", picker_low, weighted_rest, preferred_element_type=jnp.float32
    )
    layer_out = (hidden + RESIDUAL * mixture).astype(jnp.bfloat16)
    grad_top = out_grad.astype(jnp.float32)
    moe_slot = RESIDUAL * jnp.einsum(
        "sejq,sqd->sejd", picker_low, out_grad, preferred_element_type=jnp.float32
    )
    gate_grad_slot = jnp.sum(returned_f * moe_slot, axis=-1)
    send_grad = (gate_slot[..., None] * moe_slot).astype(jnp.bfloat16)
    gate_grads = jnp.einsum("sejq,sej->sqe", picker, gate_grad_slot, precision=HIGHEST)
    logit_grad = gate_probs * (
        gate_grads - jnp.sum(gate_probs * gate_grads, axis=-1, keepdims=True)
    )
    logit_low = logit_grad.astype(jnp.bfloat16)
    grad_rows = lax.all_to_all(send_grad, "ctx", split_axis=1, concat_axis=2, tiled=True)
    gate_up = jnp.einsum("serd,def->serf", received, w_gate_up, preferred_element_type=jnp.float32)
    gate_part = gate_up[..., :FF]
    up_part = gate_up[..., FF:]
    sigmoid = jax.nn.sigmoid(gate_part)
    swish_out = gate_part * sigmoid
    active_low = (swish_out * up_part).astype(jnp.bfloat16)
    active_grad = jnp.einsum(
        "serd,def->serf", grad_rows, w_down, preferred_element_type=jnp.float32
    )
    gate_grad = active_grad * up_part * (sigmoid * (1.0 + gate_part * (1.0 - sigmoid)))
    up_grad = active_grad * swish_out
    gate_up_grad = jnp.concatenate([gate_grad, up_grad], axis=-1).astype(jnp.bfloat16)
    row_grad = jnp.einsum(
        "serf,def->serd", gate_up_grad, w_gate_up, preferred_element_type=jnp.float32
    ).astype(jnp.bfloat16)
    gate_up_term = jnp.einsum(
        "serd,serf->def", received, gate_up_grad, preferred_element_type=jnp.float32
    )
    down_term = jnp.einsum(
        "serd,serf->def", grad_rows, active_low, preferred_element_type=jnp.float32
    )
    back_rows = lax.all_to_all(row_grad, "ctx", split_axis=2, concat_axis=1, tiled=True)
    normed_two_grad = jnp.einsum(
        "sejq,sejd->sqd", picker_low, back_rows, preferred_element_type=jnp.float32
    )
    normed_two_grad = normed_two_grad + jnp.einsum(
        "sqe,de->sqd", logit_low, w_router, preferred_element_type=jnp.float32
    )
    router_term = jnp.einsum(
        "sqd,sqe->de", second_low, logit_low, preferred_element_type=jnp.float32
    )
    hidden_norm_grad, gain_two_term = norm_back(hidden, scale_two, gain_second, normed_two_grad)
    hidden_grad = grad_top + hidden_norm_grad
    branch_low = (RESIDUAL * hidden_grad).astype(jnp.bfloat16)
    output_term = jnp.einsum(
        "sqe,sqd->ed", attended_low, branch_low, preferred_element_type=jnp.float32
    )
    attn_grad_low = jnp.einsum(
        "sqd,ed->sqe", branch_low, w_output, preferred_element_type=jnp.float32
    ).astype(jnp.bfloat16)
    attn_grad_heads = attn_grad_low.reshape(seq_count, ctx_len, KV_HEADS, group_size, HEAD_DIM)
    delta_rows = jnp.sum(
        jnp.transpose(attn_grad_heads.astype(jnp.float32), (0, 2, 3, 1, 4)) * attn_heads, axis=-1
    )
    full_keys, full_values = (
        lax.all_gather(keys, "ctx", axis=1, tiled=True),
        lax.all_gather(values, "ctx", axis=1, tiled=True),
    )
    length = ctx_size * ctx_len
    key_len = min(512, length)

    def key_step(query_acc, block_index):
        first_row = block_index * key_len

        def key_compute(acc_in):
            key_block = lax.dynamic_slice_in_dim(full_keys, first_row, key_len, 1).reshape(
                seq_count, key_len, KV_HEADS, HEAD_DIM
            )
            value_block = lax.dynamic_slice_in_dim(full_values, first_row, key_len, 1).reshape(
                seq_count, key_len, KV_HEADS, HEAD_DIM
            )
            scores = (
                jnp.einsum(
                    "sqgrd,skgd->sgrqk", grouped, key_block, preferred_element_type=jnp.float32
                )
                * 0.125
            )
            allowed = (first_row + jnp.arange(key_len, dtype=jnp.int32))[None, :] <= positions[
                :, None
            ]
            probs = jnp.where(allowed, jnp.exp(scores - log_total[..., None]), 0.0)
            probs_low = probs.astype(jnp.bfloat16)
            prob_grad = jnp.einsum(
                "sqgrd,skgd->sgrqk",
                attn_grad_heads,
                value_block,
                preferred_element_type=jnp.float32,
            )
            score_grad = (probs * (prob_grad - delta_rows[..., None])).astype(jnp.bfloat16)
            acc_out = (
                acc_in
                + jnp.einsum(
                    "sgrqk,skgd->sqgrd", score_grad, key_block, preferred_element_type=jnp.float32
                )
                * 0.125
            )
            key_part = (
                jnp.einsum(
                    "sgrqk,sqgrd->skgd", score_grad, grouped, preferred_element_type=jnp.float32
                )
                * 0.125
            )
            value_part = jnp.einsum(
                "sgrqk,sqgrd->skgd", probs_low, attn_grad_heads, preferred_element_type=jnp.float32
            )
            joined = jnp.concatenate(
                [
                    key_part.reshape(seq_count, key_len, KV_HEADS * HEAD_DIM),
                    value_part.reshape(seq_count, key_len, KV_HEADS * HEAD_DIM),
                ],
                axis=-1,
            )
            return (acc_out, joined)

        def skipped(acc_in):
            return (acc_in, jnp.zeros((seq_count, key_len, 2 * KV_HEADS * HEAD_DIM), jnp.float32))

        return lax.cond(first_row <= last_pos, key_compute, skipped, query_acc)

    start_query = jnp.zeros((seq_count, ctx_len, KV_HEADS, group_size, HEAD_DIM), jnp.float32)
    query_acc, key_terms = lax.scan(
        key_step, start_query, jnp.arange(length // key_len, dtype=jnp.int32)
    )
    all_terms = jnp.moveaxis(key_terms, 0, 1).reshape(seq_count, length, 2 * KV_HEADS * HEAD_DIM)
    owned_terms = lax.psum_scatter(
        all_terms.astype(jnp.bfloat16), "ctx", scatter_dimension=1, tiled=True
    ).astype(jnp.float32)
    key_grad_low = (
        rotate(
            owned_terms[..., : KV_HEADS * HEAD_DIM].reshape(seq_count, ctx_len, KV_HEADS, HEAD_DIM),
            positions,
            -1.0,
        )
        .reshape(seq_count, ctx_len, KV_HEADS * HEAD_DIM)
        .astype(jnp.bfloat16)
    )
    value_grad_low = owned_terms[..., KV_HEADS * HEAD_DIM :].astype(jnp.bfloat16)
    query_grad_low = (
        rotate(query_acc.reshape(seq_count, ctx_len, HEADS, HEAD_DIM), positions, -1.0)
        .reshape(seq_count, ctx_len, HEADS * HEAD_DIM)
        .astype(jnp.bfloat16)
    )
    query_term = jnp.einsum(
        "sqd,sqe->de", first_low, query_grad_low, preferred_element_type=jnp.float32
    )
    key_term = jnp.einsum(
        "sqd,sqe->de", first_low, key_grad_low, preferred_element_type=jnp.float32
    )
    value_term = jnp.einsum(
        "sqd,sqe->de", first_low, value_grad_low, preferred_element_type=jnp.float32
    )
    normed_one_grad = jnp.einsum(
        "sqe,de->sqd", query_grad_low, w_query, preferred_element_type=jnp.float32
    )
    normed_one_grad = normed_one_grad + jnp.einsum(
        "sqe,de->sqd", key_grad_low, w_key, preferred_element_type=jnp.float32
    )
    normed_one_grad = normed_one_grad + jnp.einsum(
        "sqe,de->sqd", value_grad_low, w_value, preferred_element_type=jnp.float32
    )
    input_norm_grad, gain_one_term = norm_back(inputs, scale_one, gain_first, normed_one_grad)
    tokens_grad = hidden_grad + input_norm_grad
    shards = (
        lax.psum_scatter(
            gain_one_term.astype(jnp.bfloat16), "fsdp", scatter_dimension=0, tiled=True
        ).astype(jnp.float32),
        lax.psum_scatter(
            query_term.astype(jnp.bfloat16), "fsdp", scatter_dimension=0, tiled=True
        ).astype(jnp.float32),
        lax.psum_scatter(
            key_term.astype(jnp.bfloat16), "fsdp", scatter_dimension=0, tiled=True
        ).astype(jnp.float32),
        lax.psum_scatter(
            value_term.astype(jnp.bfloat16), "fsdp", scatter_dimension=0, tiled=True
        ).astype(jnp.float32),
        lax.psum_scatter(
            output_term.astype(jnp.bfloat16), "fsdp", scatter_dimension=0, tiled=True
        ).astype(jnp.float32),
        lax.psum_scatter(
            gain_two_term.astype(jnp.bfloat16), "fsdp", scatter_dimension=0, tiled=True
        ).astype(jnp.float32),
        lax.psum_scatter(
            router_term.astype(jnp.bfloat16), "fsdp", scatter_dimension=0, tiled=True
        ).astype(jnp.float32),
        lax.psum_scatter(
            gate_up_term.astype(jnp.bfloat16), "fsdp", scatter_dimension=0, tiled=True
        ).astype(jnp.float32),
        lax.psum_scatter(
            down_term.astype(jnp.bfloat16), "fsdp", scatter_dimension=0, tiled=True
        ).astype(jnp.float32),
    )
    gain_one_out, query_out, key_out, value_out, output_out, gain_two_out, router_out = (
        lax.psum(shards[0].astype(jnp.bfloat16), "ctx").astype(jnp.float32),
        lax.psum(shards[1].astype(jnp.bfloat16), "ctx").astype(jnp.float32),
        lax.psum(shards[2].astype(jnp.bfloat16), "ctx").astype(jnp.float32),
        lax.psum(shards[3].astype(jnp.bfloat16), "ctx").astype(jnp.float32),
        lax.psum(shards[4].astype(jnp.bfloat16), "ctx").astype(jnp.float32),
        lax.psum(shards[5].astype(jnp.bfloat16), "ctx").astype(jnp.float32),
        lax.psum(shards[6].astype(jnp.bfloat16), "ctx").astype(jnp.float32),
    )
    gate_up_out = shards[7]
    down_out = shards[8]
    return (
        layer_out,
        tokens_grad,
        gain_one_out,
        query_out,
        key_out,
        value_out,
        output_out,
        gain_two_out,
        router_out,
        gate_up_out,
        down_out,
    )


def solution(mesh):
    in_specs = (
        P("fsdp", "ctx", None),
        P("fsdp"),
        P("fsdp", None),
        P("fsdp", None),
        P("fsdp", None),
        P("fsdp", None),
        P("fsdp"),
        P("fsdp", None),
        P("fsdp", "ctx", None),
        P("fsdp", "ctx", None),
        P("fsdp", "ctx", None),
        P("fsdp", "ctx", None),
    )
    out_specs = (
        P("fsdp", "ctx", None),
        P("fsdp", "ctx", None),
        P("fsdp"),
        P("fsdp", None),
        P("fsdp", None),
        P("fsdp", None),
        P("fsdp", None),
        P("fsdp"),
        P("fsdp", None),
        P("fsdp", "ctx", None),
        P("fsdp", "ctx", None),
    )
    return jax.shard_map(
        per_device, mesh=mesh, in_specs=in_specs, out_specs=out_specs, check_vma=False
    )
```

profile of v0, /device:TPU:0, one launch (start us, length us, event | category | flops | bytes accessed | tf_op | source)
XLA Modules:
  0.0 887.3 jit_solution(4661011510900577573)
XLA Ops:
  10.1 12.6 %all-gather.1 = bf16[4,1,256]{2,1,0:T(2,128)(2,1)S(1)} all-gather(bf16[1,1,256]{2,1,0:T(2,128)(2,1)S(1)} %reshape.693), channel_id=1, replica_groups=mesh['ctx'=8,'fsdp'=4] {'fsdp'}, dimensions={0}, use_global_device_ids=true | all-gather | bytes 2560 | tf_op jit(solution)/shard_map/all_gather | solution.py:63
  24.6 15.7 %all-gather.12.cloned.1.call-done = bf16[1024,512]{1,0:T(8,128)(2,1)} async-done(((bf16[256,512]{1,0:T(8,128)(2,1)}), bf16[1024,512]{1,0:T(8,128)(2,1)}) %all-gather.12.cloned.1.call-update) | async-done | bytes 1048592 | tf_op jit(solution)/shard_map/all_gather | solution.py:65
  43.1 26.1 %all-gather.18.cloned.1.call-done = bf16[1024,512]{1,0:T(8,128)(2,1)} async-done(((bf16[256,512]{1,0:T(8,128)(2,1)}), bf16[1024,512]{1,0:T(8,128)(2,1)}) %all-gather.18.cloned.1.call-update) | async-done | bytes 1048592 | tf_op jit(solution)/shard_map/all_gather | solution.py:66
  74.4 9.5 %all-gather.2 = bf16[4,1,256]{2,1,0:T(2,128)(2,1)S(1)} all-gather(bf16[1,1,256]{2,1,0:T(2,128)(2,1)S(1)} %reshape.695), channel_id=1, replica_groups=mesh['ctx'=8,'fsdp'=4] {'fsdp'}, dimensions={0}, use_global_device_ids=true | all-gather | bytes 2560 | tf_op jit(solution)/shard_map/all_gather | solution.py:68
  84.3 31.7 %all-gather.16.cloned.1.call-done = bf16[1024,1024]{1,0:T(8,128)(2,1)} async-done(((bf16[256,1024]{1,0:T(8,128)(2,1)}), bf16[1024,1024]{1,0:T(8,128)(2,1)}) %all-gather.16.cloned.1.call-update) | async-done | bytes 2097168 | tf_op jit(solution)/shard_map/all_gather | solution.py:64
  115.9 2.9 copy.109
  119.7 20.8 %all-gather.14.cloned.1.call-done = bf16[1,1024,512]{1,2,0:T(8,128)(2,1)} async-done(((bf16[1,128,512]{1,2,0:T(8,128)(2,1)}), bf16[1,1024,512]{1,2,0:T(8,128)(2,1)}) %all-gather.14.cloned.1.call-update) | async-done | bytes 1048592 | tf_op jit(solution)/shard_map/all_gather | solution.py:100
  140.5 25.7 %all-gather.26.cloned.1.call-done = bf16[1024,512]{1,0:T(8,128)(2,1)} async-done(((bf16[128,512]{1,0:T(8,128)(2,1)}), bf16[1024,512]{1,0:T(8,128)(2,1)}) %all-gather.26.cloned.1.call-update) | async-done | bytes 1048592 | tf_op jit(solution)/shard_map/all_gather | solution.py:101
  166.2 12.9 %conditional.2 = (f32[1,8,2,128]{3,2,1,0:T(2,128)}, f32[1,8,2,128,64]{3,4,2,1,0:T(8,128)S(1)}, f32[1,8,2,128]{3,2,1,0:T(2,128)S(1)}) conditional(s32[]{:T(128)} %convert_element_type.350, () %tuple.30, (s32[128]{0:T(128)S(1)}, bf16[1,1024,512]{1,2,0:T(8,128)(2,1)}, bf16[1,128,8,2,64]{1,4,3,2,0:T(8,128)(2,1)S(1)}, ...), branch_computations={%region_1.0_spmd.clone, %region_2.5_spmd.clone} | conditional | flops 560072704 | bytes 68493904 | solution.py:130
  166.3 2.7 fusion.42
  169.0 2.8 fusion.41
  172.8 5.6 fusion.47
  179.9 33.4 %all-gather.20.cloned.1.call-done = bf16[1024,1024]{1,0:T(8,128)(2,1)} async-done(((bf16[256,1024]{1,0:T(8,128)(2,1)}), bf16[1024,1024]{1,0:T(8,128)(2,1)}) %all-gather.20.cloned.1.call-update) | async-done | bytes 2097168 | tf_op jit(solution)/shard_map/all_gather | solution.py:67
  216.4 30.3 %all_to_all.54 = bf16[1,16,64,1024]{3,2,0,1:T(8,128)(2,1)S(1)} all-to-all(bf16[1,16,64,1024]{3,2,0,1:T(8,128)(2,1)S(1)} %convert_bitcast_fusion.4), channel_id=1, replica_groups=mesh['ctx'=8,'fsdp'=4] {'ctx'}, dimensions={1} | all-to-all | bytes 4194304 | tf_op jit(solution)/shard_map/all_to_all | solution.py:159
  246.8 48.2 %all-gather.22.cloned.1.call-done = bf16[1024,2,1024]{2,0,1:T(8,128)(2,1)} async-done(((bf16[256,2,1024]{2,0,1:T(8,128)(2,1)}), bf16[1024,2,1024]{2,0,1:T(8,128)(2,1)}) %all-gather.22.cloned.1.call-update) | async-done | bytes 4194320 | tf_op jit(solution)/shard_map/all_gather | solution.py:70
  295.1 4.5 convolution_bitcast_fusion
  303.3 38.1 %all-gather.24.cloned.1.call-done = bf16[1024,2,512]{2,0,1:T(8,128)(2,1)} async-done(((bf16[256,2,512]{2,0,1:T(8,128)(2,1)}), bf16[1024,2,512]{2,0,1:T(8,128)(2,1)}) %all-gather.24.cloned.1.call-update) | async-done | bytes 2097168 | tf_op jit(solution)/shard_map/all_gather | solution.py:71
  341.4 3.2 convert_bitcast_fusion.3
  344.6 3.5 copy.118
  348.1 4.5 all-to-all-start.1
  352.6 13.1 %all_gather.45 = bf16[1024,16]{0,1:T(8,128)(2,1)S(1)} all-gather(bf16[256,16]{0,1:T(8,128)(2,1)S(1)} %copy-done.40), channel_id=1, replica_groups=mesh['ctx'=8,'fsdp'=4] {'fsdp'}, dimensions={0}, use_global_device_ids=true | all-gather | bytes 40960 | tf_op jit(solution)/shard_map/all_gather | solution.py:69
  366.0 13.2 %all-to-all-done.1 = bf16[1,2,512,1024]{3,1,0,2:T(2,128)(2,1)} async-done(((bf16[1,2,512,1024]{3,1,0,2:T(2,128)(2,1)}), bf16[1,2,512,1024]{3,1,0,2:T(2,128)(2,1)}, u32[]{:S(2)}, u32[]{:S(2)}) %all-to-all-start.1) | async-done | bytes 2097184 | tf_op jit(solution)/shard_map/all_to_all | solution.py:165
  379.2 2.4 copy.119
  385.7 29.1 %all_to_all.55 = bf16[1,16,64,1024]{3,2,0,1:T(8,128)(2,1)S(1)} all-to-all(bf16[1,16,64,1024]{3,2,0,1:T(8,128)(2,1)S(1)} %fusion.56), channel_id=1, replica_groups=mesh['ctx'=8,'fsdp'=4] {'ctx'}, dimensions={1} | all-to-all | bytes 4194304 | tf_op jit(solution)/shard_map/all_to_all | solution.py:188
  415.0 2.7 copy-done.13
  419.9 2.4 convert_bitcast_fusion.2
  422.3 3.5 copy.124
  425.8 3.6 all-to-all-start.3
  429.4 8.4 reduce-scatter.9.cloned.1.call-start
  440.1 15.8 %all-to-all-done.3 = bf16[1,2,512,1024]{3,1,0,2:T(2,128)(2,1)S(1)} async-done(((bf16[1,2,512,1024]{3,1,0,2:T(2,128)(2,1)}), bf16[1,2,512,1024]{3,1,0,2:T(2,128)(2,1)S(1)}, u32[]{:S(2)}, u32[]{:S(2)}) %all-to-all-start.3) | async-done | bytes 2097184 | tf_op jit(solution)/shard_map/all_to_all | solution.py:210
  461.9 14.2 %while.16 = (s32[]{:T(128)}, f32[1,128,8,2,64]{1,4,3,2,0:T(8,128)S(1)}, bf16[2,1,512,1024]{3,2,0,1:T(8,128)(2,1)}, s32[2]{0:T(128)S(1)}, s32[]{:T(128)}, /*index...) while((s32[]{:T(128)}, ...), condition=%wide.region_17.18_spmd.clone, body=%wide.region_14.17_spmd.clone.sunk | while | flops 684524160 | bytes 32209220 | solution.py:299
  463.1 8.4 conditional.5
  465.9 2.4 fusion.3
  481.3 41.4 %reduce-scatter.9.cloned.1.call-done = bf16[1,128,1024]{2,1,0:T(8,128)(2,1)} async-done(((bf16[1,1024,1024]{2,1,0:T(8,128)(2,1)}), bf16[1,128,1024]{2,1,0:T(8,128)(2,1)}) %reduce-scatter.9.cloned.1.call-update) | async-done | bytes 262160 | tf_op jit(solution)/shard_map/reduce_scatter | solution.py:303
  527.1 4.2 convert_bitcast_fusion.1
  532.8 36.3 %reduce-scatter.11.cloned.1.call-done = bf16[256,1024]{1,0:T(8,128)(2,1)} async-done(((bf16[1024,1024]{1,0:T(8,128)(2,1)}), bf16[256,1024]{1,0:T(8,128)(2,1)}) %reduce-scatter.11.cloned.1.call-update) | async-done | bytes 524304 | tf_op jit(solution)/shard_map/reduce_scatter | solution.py:345
  569.1 45.2 %reduce-scatter.17.cloned.1.call-done = bf16[256,1024]{1,0:T(8,128)(2,1)} async-done(((bf16[1024,1024]{1,0:T(8,128)(2,1)}), bf16[256,1024]{1,0:T(8,128)(2,1)}) %reduce-scatter.17.cloned.1.call-update) | async-done | bytes 524304 | tf_op jit(solution)/shard_map/reduce_scatter | solution.py:354
  614.3 29.3 %reduce-scatter.13.cloned.1.call-done = bf16[256,512]{1,0:T(8,128)(2,1)} async-done(((bf16[1024,512]{1,0:T(8,128)(2,1)}), bf16[256,512]{1,0:T(8,128)(2,1)}) %reduce-scatter.13.cloned.1.call-update) | async-done | bytes 262160 | tf_op jit(solution)/shard_map/reduce_scatter | solution.py:348
  643.5 28.7 %reduce-scatter.15.cloned.1.call-done = bf16[256,512]{1,0:T(8,128)(2,1)} async-done(((bf16[1024,512]{1,0:T(8,128)(2,1)}), bf16[256,512]{1,0:T(8,128)(2,1)}) %reduce-scatter.15.cloned.1.call-update) | async-done | bytes 262160 | tf_op jit(solution)/shard_map/reduce_scatter | solution.py:351
  672.5 6.3 convert_bitcast_fusion
  680.8 3.1 fusion.63
  686.8 29.7 %reduce-scatter.23.cloned.1.call-done = bf16[256,2,512]{0,2,1:T(8,128)(2,1)} async-done(((bf16[1024,2,512]{0,2,1:T(8,128)(2,1)}), bf16[256,2,512]{0,2,1:T(8,128)(2,1)}) %reduce-scatter.23.cloned.1.call-update) | async-done | bytes 524304 | tf_op jit(solution)/shard_map/reduce_scatter | solution.py:366
  720.2 10.2 %all-reduce.4 = (bf16[1024]{0:T(1024)(128)(2,1)S(1)}, bf16[1024]{0:T(1024)(128)(2,1)S(1)}) all-reduce(bf16[1024]{0:T(1024)(128)(2,1)S(1)} %get-tuple-element.279, bf16[1024]{0:T(1024)(128)(2,1)S(1)} %copy-done.39), channel_id=4, replica_groups=mesh['ctx'=8,'fsdp'=4] {'fsdp'}, use_global_device_ids=true, to_apply=%region_21.22.clone | all-reduce | flops 2048 | bytes 8192
  730.5 7.2 reduce-scatter.19.cloned.1.call-done
  737.6 13.0 %all-reduce.2 = (bf16[256]{0:T(256)(128)(2,1)S(1)}, bf16[256]{0:T(256)(128)(2,1)S(1)}, bf16[256,16]{0,1:T(8,128)(2,1)S(1)}) all-reduce(bf16[256]{0:T(256)(128)(2,1)S(1)} %dynamic-slice.1, bf16[256]{0:T(256)(128)(2,1)S(1)} %dynamic-slice.3, ...), channel_id=1, replica_groups=mesh['ctx'=8,'fsdp'=4] {'ctx'}, use_global_device_ids=true, to_apply=%region_22.23 | all-reduce | flops 4608 | bytes 18432 | tf_op jit(solution)/shard_map/psum | solution.py:371
  753.3 45.1 %all-reduce.7.cloned.1.call-done = (bf16[256,1024]{1,0:T(8,128)(2,1)}, bf16[256,512]{1,0:T(8,128)(2,1)}, bf16[256,512]{1,0:T(8,128)(2,1)}, bf16[256,1024]{1,0:T(8,128)(2,1)}) async-done(((bf16[256,1024]{1,0:T(8,128)(2,1)}, bf16[256,512]{1,0:T(8,128)(2,1)}, bf16[256,512]{1,0:T(8,128)(2,1)}, bf16[256,1024]{1,0:T(8,128)(2,1)}), (bf16[256,1024]{1,0:T(8,128)(2,1)}, bf16[256,512]{1,0:T(8,128)(2,1)}, ...) | async-done | bytes 1572880 | tf_op jit(solution)/shard_map/psum | solution.py:372
  804.4 72.4 %reduce-scatter.21.cloned.1.call-done = bf16[256,2,1024]{0,2,1:T(8,128)(2,1)} async-done(((bf16[1024,2,1024]{0,2,1:T(8,128)(2,1)}), bf16[256,2,1024]{0,2,1:T(8,128)(2,1)}) %reduce-scatter.21.cloned.1.call-update) | async-done | bytes 1048592 | tf_op jit(solution)/shard_map/reduce_scatter | solution.py:363
  876.7 3.8 copy.132
  (236 shorter events, 76.3 us)
Async XLA Ops:
  7.2 34.6 %copy-start.3 = (bf16[1,128,1024]{2,1,0:T(8,128)(2,1)S(1)}, bf16[1,128,1024]{2,1,0:T(8,128)(2,1)}, u32[]{:S(2)}) copy-start(bf16[1,128,1024]{2,1,0:T(8,128)(2,1)} %param.18) | copy-start | bytes 786436
  7.2 33.1 %all-gather.12.cloned.1.call-start = ((), (), s32[]{:S(2)}) async-start(), calls=%async_computation.12 | async-start | bytes 1310720 | tf_op jit(solution)/shard_map/all_gather | solution.py:65
  7.9 61.3 %all-gather.18.cloned.1.call-start = ((), (), s32[]{:S(2)}) async-start(), calls=%async_computation.15 | async-start | bytes 1310720 | tf_op jit(solution)/shard_map/all_gather | solution.py:66
  8.7 107.2 %all-gather.16.cloned.1.call-start = ((), (), s32[]{:S(2)}) async-start(), calls=%async_computation.14 | async-start | bytes 2621440 | tf_op jit(solution)/shard_map/all_gather | solution.py:64
  9.4 131.1 %all-gather.14.cloned.1.call-start = ((), (), s32[]{:S(2)}) async-start(), calls=%async_computation.13 | async-start | bytes 1179648 | tf_op jit(solution)/shard_map/all_gather | solution.py:100
  24.6 94.9 %copy-start.29 = (f32[128,32]{0,1:T(8,128)}, f32[128,32]{0,1:T(8,128)S(1)}, u32[]{:S(2)}) copy-start(f32[128,32]{0,1:T(8,128)S(1)} %get-tuple-element.332) | copy-start | bytes 49156
  41.8 30.4 %copy-start.22 = (bf16[256,2,1024]{2,1,0:T(2,128)(2,1)S(1)}, bf16[256,2,1024]{2,1,0:T(2,128)(2,1)}, u32[]{:S(2)}) copy-start(bf16[256,2,1024]{2,1,0:T(2,128)(2,1)} %param.26) | copy-start | bytes 3145732
  43.1 123.2 %all-gather.26.cloned.1.call-start = ((), (), s32[]{:S(2)}) async-start(), calls=%async_computation.27 | async-start | bytes 1179648 | tf_op jit(solution)/shard_map/all_gather | solution.py:101
  71.5 141.8 %all-gather.20.cloned.1.call-start = ((), (), s32[]{:S(2)}) async-start(), calls=%async_computation.16 | async-start | bytes 2621440 | tf_op jit(solution)/shard_map/all_gather | solution.py:67
  72.1 2.3 copy-start.44
  72.1 11.8 %copy-start.41 = (s32[1,128,8]{1,2,0:T(8,128)S(1)}, s32[1,128,8]{1,2,0:T(8,128)}, u32[]{:S(2)}) copy-start(s32[1,128,8]{1,2,0:T(8,128)} %param.28) | copy-start | bytes 12292
  72.1 222.9 %all-gather.22.cloned.1.call-start = ((), (), s32[]{:S(2)}) async-start(), calls=%async_computation.17 | async-start | bytes 5242880 | tf_op jit(solution)/shard_map/all_gather | solution.py:70
  73.5 267.9 %all-gather.24.cloned.1.call-start = ((), (), s32[]{:S(2)}) async-start(), calls=%async_computation.18 | async-start | bytes 2621440 | tf_op jit(solution)/shard_map/all_gather | solution.py:71
  84.3 372.3 %copy-start.31 = (f32[16,128]{1,0:T(8,128)}, f32[16,128]{1,0:T(8,128)S(1)}, u32[]{:S(2)}) copy-start(f32[16,128]{1,0:T(8,128)S(1)} %copy.112) | copy-start | bytes 24580
  169.0 3.3 copy-start.2
  169.0 3.3 copy-start.16
  179.1 34.2 %copy-start.10 = (f32[1,8,2,128,64]{3,4,2,1,0:T(8,128)}, f32[1,8,2,128,64]{3,4,2,1,0:T(8,128)S(1)}, u32[]{:S(2)}) copy-start(f32[1,8,2,128,64]{3,4,2,1,0:T(8,128)S(1)} %get-tuple-element.120) | copy-start | bytes 1572868
  179.9 36.5 %copy-start.17 = (bf16[1,8,2,128,64]{3,4,2,1,0:T(8,128)(2,1)}, bf16[1,8,2,128,64]{3,4,2,1,0:T(8,128)(2,1)S(1)}, u32[]{:S(2)}) copy-start(bf16[1,8,2,128,64]{3,4,2,1,0:T(8,128)(2,1)S(1)} %fusion.128) | copy-start | bytes 786436
  215.5 242.5 %copy-start.4 = (f32[1,128,1024]{2,1,0:T(8,128)}, f32[1,128,1024]{2,1,0:T(8,128)S(1)}, u32[]{:S(2)}) copy-start(f32[1,128,1024]{2,1,0:T(8,128)S(1)} %get-tuple-element.334) | copy-start | bytes 1572868
  246.8 52.8 %copy-start.19 = (bf16[1,8,2,64,1024]{4,3,1,2,0:T(8,128)(2,1)}, bf16[1,8,2,64,1024]{4,3,1,2,0:T(8,128)(2,1)S(1)}, u32[]{:S(2)}) copy-start(bf16[1,8,2,64,1024]{4,3,1,2,0:T(8,128)(2,1)S(1)} %copy.115) | copy-start | bytes 6291460
  348.1 4.5 copy-start.40
  348.1 31.1 %all-to-all-start.1 = ((bf16[1,2,512,1024]{3,1,0,2:T(2,128)(2,1)}), bf16[1,2,512,1024]{3,1,0,2:T(2,128)(2,1)}, u32[]{:S(2)}, u32[]{:S(2)}) async-start(bf16[1,2,512,1024]{3,1,0,2:T(2,128)(2,1)} %copy.118), calls=%async_computation.1 | async-start | bytes 4194304 | tf_op jit(solution)/shard_map/all_to_all | solution.py:165
  379.2 2.4 copy-start.23
  385.6 29.3 %copy-start.43 = (bf16[1024,2,512]{2,0,1:T(8,128)(2,1)S(1)}, bf16[1024,2,512]{2,0,1:T(8,128)(2,1)}, u32[]{:S(2)}) copy-start(bf16[1024,2,512]{2,0,1:T(8,128)(2,1)} %all-gather.24.cloned.1.call-done) | copy-start | bytes 6291460
  414.8 2.9 copy-start.13
  415.0 4.7 copy-start.20
  419.7 2.6 copy-start.46
  419.7 2.6 copy-start.48
  425.8 30.2 %all-to-all-start.3 = ((bf16[1,2,512,1024]{3,1,0,2:T(2,128)(2,1)}), bf16[1,2,512,1024]{3,1,0,2:T(2,128)(2,1)S(1)}, u32[]{:S(2)}, u32[]{:S(2)}) async-start(bf16[1,2,512,1024]{3,1,0,2:T(2,128)(2,1)} %copy.124), calls=%async_computation.3 | async-start | bytes 4194304 | tf_op jit(solution)/shard_map/all_to_all | solution.py:210
  429.4 93.3 %reduce-scatter.9.cloned.1.call-start = ((), (), s32[]{:S(2)}) async-start(), calls=%async_computation.19 | async-start | bytes 2359296 | tf_op jit(solution)/shard_map/reduce_scatter | solution.py:303
  440.1 17.0 %copy-start.37 = (bf16[128,16]{0,1:T(8,128)(2,1)}, bf16[128,16]{0,1:T(8,128)(2,1)S(1)}, u32[]{:S(2)}) copy-start(bf16[128,16]{0,1:T(8,128)(2,1)S(1)} %fusion.134) | copy-start | bytes 12292
  476.1 93.0 %reduce-scatter.11.cloned.1.call-start = ((), (), s32[]{:S(2)}) async-start(), calls=%async_computation.20 | async-start | bytes 2621440 | tf_op jit(solution)/shard_map/reduce_scatter | solution.py:345
  476.9 2.2 copy-start.9
  479.1 135.2 %reduce-scatter.17.cloned.1.call-start = ((), (), s32[]{:S(2)}) async-start(), calls=%async_computation.23 | async-start | bytes 2621440 | tf_op jit(solution)/shard_map/reduce_scatter | solution.py:354
  481.3 162.3 %reduce-scatter.13.cloned.1.call-start = ((), (), s32[]{:S(2)}) async-start(), calls=%async_computation.21 | async-start | bytes 1310720 | tf_op jit(solution)/shard_map/reduce_scatter | solution.py:348
  522.7 2.8 copy-start.25
  525.4 146.8 %reduce-scatter.15.cloned.1.call-start = ((), (), s32[]{:S(2)}) async-start(), calls=%async_computation.22 | async-start | bytes 1310720 | tf_op jit(solution)/shard_map/reduce_scatter | solution.py:351
  527.0 189.5 %reduce-scatter.23.cloned.1.call-start = ((), (), s32[]{:S(2)}) async-start(), calls=%async_computation.26 | async-start | bytes 2621440 | tf_op jit(solution)/shard_map/reduce_scatter | solution.py:366
  531.3 141.2 %copy-start.47 = (bf16[2,512,512]{2,1,0:T(8,128)(2,1)S(1)}, bf16[2,512,512]{2,1,0:T(8,128)(2,1)}, u32[]{:S(2)}) copy-start(bf16[2,512,512]{2,1,0:T(8,128)(2,1)} %copy-done.46) | copy-start | bytes 3145732
  531.3 206.3 %reduce-scatter.19.cloned.1.call-start = ((), (), s32[]{:S(2)}) async-start(), calls=%async_computation.24 | async-start | bytes 40960 | tf_op jit(solution)/shard_map/reduce_scatter | solution.py:360
  532.8 265.6 %all-reduce.7.cloned.1.call-start = ((), (), s32[]{:S(2)}) async-start(), calls=%async_computation.28 | async-start | bytes 3145728 | tf_op jit(solution)/shard_map/psum | solution.py:372
  672.2 204.5 %reduce-scatter.21.cloned.1.call-start = ((), (), s32[]{:S(2)}) async-start(), calls=%async_computation.25 | async-start | bytes 5242880 | tf_op jit(solution)/shard_map/reduce_scatter | solution.py:363
  680.7 3.5 copy-start.1
  680.8 3.6 copy-start.5
  686.0 32.6 %copy-start.14 = (bf16[1024,512]{1,0:T(8,128)(2,1)S(1)}, bf16[1024,512]{1,0:T(8,128)(2,1)}, u32[]{:S(2)}) copy-start(bf16[1024,512]{1,0:T(8,128)(2,1)} %all-gather.12.cloned.1.call-done) | copy-start | bytes 3145732
  686.8 32.3 %copy-start.15 = (bf16[1024,512]{1,0:T(8,128)(2,1)S(1)}, bf16[1024,512]{1,0:T(8,128)(2,1)}, u32[]{:S(2)}) copy-start(bf16[1024,512]{1,0:T(8,128)(2,1)} %all-gather.18.cloned.1.call-done) | copy-start | bytes 3145732
  798.4 4.0 copy-start.33
  798.4 4.9 copy-start.27
  (20 other events, 29.3 us)
Sparse Core Ops, SparseCore 0:
  9.6 30.6 all-gather.11
  41.9 27.3 all-gather.17
  70.8 45.0 all-gather.15
  118.2 22.2 all-gather.13
  142.8 23.3 all-gather.25
  167.7 45.6 all-gather.19
  215.5 79.5 all-gather.21
  297.2 44.1 all-gather.23
  476.2 46.4 reduce-scatter.8
  525.4 43.6 reduce-scatter.10
  571.4 42.8 reduce-scatter.16
  617.0 26.4 reduce-scatter.12
  646.4 25.7 reduce-scatter.14
  674.4 42.1 reduce-scatter.22
  719.2 18.4 reduce-scatter.18
  741.0 57.3 all-reduce.6
  800.5 76.1 reduce-scatter.20
where the time goes:
time: 896 us; the launch traced here: 887 us
  waiting for transfers between devices  607 us (68%)
  blocking collectives  118 us (13%)
  matrix products  62.5 us (7%)
  local copies, waits for them, and re-layouts  45.1 us (5%)
  other arithmetic  20.8 us (2%)
  starting transfers between devices  17.3 us (2%)
  between operations  15.6 us (2%)
    reduce_scatter x1, waiting for transfers between devices, per_device(): lax.psum_scatter(gate_up_term.astype(jnp.bfloat16), 'fsdp', scatter_dimen...  72.4 us
    all_gather x1, waiting for transfers between devices, per_device(): lax.all_gather(expert_in, 'fsdp', axis=0, tiled=True)  48.2 us
    reduce_scatter x1, waiting for transfers between devices, per_device(): lax.psum_scatter(output_term.astype(jnp.bfloat16), 'fsdp', scatter_dimens...  45.2 us
    psum x1, waiting for transfers between devices, per_device(): lax.psum(shards[1].astype(jnp.bfloat16), 'ctx').astype(jnp.float32)  45.1 us
    reduce_scatter x1, waiting for transfers between devices, per_device(): lax.psum_scatter(all_terms.astype(jnp.bfloat16), 'ctx', scatter_dimension...  41.4 us
    all_gather x1, waiting for transfers between devices, per_device(): lax.all_gather(expert_out, 'fsdp', axis=0, tiled=True)  38.1 us
    reduce_scatter x1, waiting for transfers between devices, per_device(): lax.psum_scatter(query_term.astype(jnp.bfloat16), 'fsdp', scatter_dimensi...  36.3 us
    all_gather x1, waiting for transfers between devices, per_device(): lax.all_gather(output_weight, 'fsdp', axis=0, tiled=True)  33.4 us
  transfers between devices with their start and end apart: 19, of which 19 were waited for; matrix products, arithmetic and copies ran while one was open for 9% of the time, Pallas kernels for 0%

commit v1 on v0

v1 whole, which is shorter than its diff:
```python
import jax
import jax.numpy as jnp
from jax import lax
from jax.experimental import pallas as pl
from jax.experimental.pallas import tpu as pltpu
from jax.sharding import PartitionSpec as P

HEADS = 16
KV_HEADS = 8
HEAD_DIM = 64
FF = 512
MOST = 64

EPSILON = 1e-06
RESIDUAL = 0.22
ROPE_BASE = 10000.0
BF = jnp.bfloat16
F32 = jnp.float32


def dot(a, b, dims=((1,), (0,))):
    return lax.dot_general(a, b, (dims, ((), ())), preferred_element_type=F32)


def bits_of(size):
    found, bit = [], 1
    while bit < size:
        found.append(bit)
        bit *= 2
    return [1] + found[:0:-1]


def order_of(size):
    places = [0]
    for bit in reversed(bits_of(size)):
        places = places + [place ^ bit for place in places]
    return places


def swap_ctx(value, bit, size):
    return lax.ppermute(value, "ctx", [(i, i ^ bit) for i in range(size)])


def paths_of(size):
    bits = bits_of(size)
    far = bits[1:]
    return bits, (far, far[1:] + far[:1])


def cut_of(width):
    return max(128, (width // 256) * 128)


def gather_half(value, path, bits, size):
    held = []
    for bit in list(path) + [1]:
        other = swap_ctx(value, bit, size)
        axis = sum(1 for seen in held if bits.index(seen) < bits.index(bit))
        value = jnp.stack([value, other], axis=axis)
        held.append(bit)
    return value.reshape((size,) + value.shape[len(bits):])


def gather_ctx(value, size):
    bits, paths = paths_of(size)
    cut = cut_of(value.shape[-1])
    parts = [value[..., :cut], value[..., cut:]]
    return jnp.concatenate(
        [gather_half(part, path, bits, size) for part, path in zip(parts, paths)], axis=-1
    )


def add_low(mine, other):
    return (mine.astype(F32) + other.astype(F32)).astype(BF)


def scatter_ctx(blocks, size):
    bits, paths = paths_of(size)
    half = size // 2
    blocks = add_low(blocks[:half], swap_ctx(blocks[half:], 1, size))
    cut = cut_of(blocks.shape[-1])
    done = []
    for part, path in zip((blocks[..., :cut], blocks[..., cut:]), paths):
        part = part.reshape((2,) * (len(bits) - 1) + part.shape[1:])
        left = bits[1:]
        for bit in reversed(path):
            axis = left.index(bit)
            keep = lax.index_in_dim(part, 0, axis, keepdims=False)
            send = lax.index_in_dim(part, 1, axis, keepdims=False)
            other = swap_ctx(send, bit, size)
            left = [b for b in left if b != bit]
            if left:
                part = add_low(keep, other)
            else:
                part = keep.astype(F32) + other.astype(F32)
        done.append(part)
    return jnp.concatenate(done, axis=-1)


def exchange_ctx(blocks, size):
    return [blocks[0]] + [swap_ctx(blocks[k], k, size) for k in range(1, size)]


def shift_fsdp(value, step, size):
    return lax.ppermute(value, "fsdp", [(i, (i + step) % size) for i in range(size)])


def gather_fsdp(value, size):
    if size != 4:
        return jnp.concatenate(
            [value] + [shift_fsdp(value, k, size) for k in range(1, size)], axis=0
        )
    rows = value.shape[0] // 2
    left = shift_fsdp(value, 1, size)
    right = shift_fsdp(value, -1, size)
    top = shift_fsdp(left[:rows], 1, size)
    low = shift_fsdp(right[rows:], -1, size)
    return jnp.concatenate([value, left, top, low, right], axis=0)


def scatter_fsdp(value, size):
    rows = value.shape[0] // size
    part = [value[k * rows : (k + 1) * rows] for k in range(size)]
    if size != 4:
        total = part[0]
        for k in range(1, size):
            total = total + shift_fsdp(part[k].astype(BF), -k, size).astype(F32)
        return total
    half = rows // 2
    far = part[2].astype(BF)
    top = shift_fsdp(far[:half], 1, size).astype(F32)
    low = shift_fsdp(far[half:], -1, size).astype(F32)
    zero = jnp.zeros_like(top)
    up = (part[3] + jnp.concatenate([top, zero], axis=0)).astype(BF)
    down = (part[1] + jnp.concatenate([zero, low], axis=0)).astype(BF)
    return (
        part[0]
        + shift_fsdp(up, 1, size).astype(F32)
        + shift_fsdp(down, -1, size).astype(F32)
    )


def pick(blocks, index):
    return lax.dynamic_index_in_dim(blocks, index, 0, keepdims=False)


def columns(value, start, width):
    return lax.dynamic_slice_in_dim(value, start, width, value.ndim - 1)


def forward_kernel(q_ref, k_ref, v_ref, qpos_ref, kpos_ref, low_ref, high_ref, lse_ref):
    allowed = kpos_ref[...] <= qpos_ref[...]
    keys = k_ref[...]
    values = v_ref[...]
    for head in range(q_ref.shape[1] // HEAD_DIM):
        cols = slice(head * HEAD_DIM, (head + 1) * HEAD_DIM)
        scores = dot(q_ref[:, cols], keys, ((1,), (1,))) * 0.125
        scores = jnp.where(allowed, scores, -1e30)
        top = jnp.max(scores, axis=-1, keepdims=True)
        weights = jnp.exp(scores - top)
        total = jnp.sum(weights, axis=-1, keepdims=True)
        out = dot(weights.astype(BF), values) / total
        high_ref[:, cols] = out
        low_ref[:, cols] = out.astype(BF)
        lse_ref[:, head : head + 1] = top + jnp.log(total)


def attend(queries, keys, values, qpos, kpos):
    length, wide = queries.shape
    rows = min(256, length)
    heads = wide // HEAD_DIM
    whole = lambda i: (0, 0)
    block = lambda i: (i, 0)
    return pl.pallas_call(
        forward_kernel,
        grid=(length // rows,),
        in_specs=[
            pl.BlockSpec((rows, wide), block),
            pl.BlockSpec((length, HEAD_DIM), whole),
            pl.BlockSpec((length, HEAD_DIM), whole),
            pl.BlockSpec((rows, 1), block),
            pl.BlockSpec((1, length), whole),
        ],
        out_specs=[
            pl.BlockSpec((rows, wide), block),
            pl.BlockSpec((rows, wide), block),
            pl.BlockSpec((rows, heads), block),
        ],
        out_shape=[
            jax.ShapeDtypeStruct((length, wide), BF),
            jax.ShapeDtypeStruct((length, wide), F32),
            jax.ShapeDtypeStruct((length, heads), F32),
        ],
        name="attend",
    )(queries, keys, values, qpos, kpos)


def turn_back(grad, cos, sin):
    middle = HEAD_DIM // 2
    swapped = jnp.concatenate([grad[:, middle:], -grad[:, :middle]], axis=-1)
    return grad * cos + swapped * sin


def backward_kernel(
    q_ref, k_ref, v_ref, qpos_ref, kpos_ref, out_ref, lse_ref, do_ref, qcos_ref, qsin_ref,
    kcos_ref, ksin_ref, dq_ref, dkv_ref, dk_acc, dv_acc,
):
    step = pl.program_id(0)

    @pl.when(step == 0)
    def _():
        dk_acc[...] = jnp.zeros_like(dk_acc)
        dv_acc[...] = jnp.zeros_like(dv_acc)

    allowed = kpos_ref[...] <= qpos_ref[...]
    keys = k_ref[...]
    values = v_ref[...]
    for head in range(q_ref.shape[1] // HEAD_DIM):
        cols = slice(head * HEAD_DIM, (head + 1) * HEAD_DIM)
        query = q_ref[:, cols]
        grad = do_ref[:, cols]
        delta = jnp.sum(grad.astype(F32) * out_ref[:, cols], axis=-1, keepdims=True)
        scores = dot(query, keys, ((1,), (1,))) * 0.125
        probs = jnp.where(allowed, jnp.exp(scores - lse_ref[:, head : head + 1]), 0.0)
        prob_grad = dot(grad, values, ((1,), (1,)))
        score_grad = (probs * (prob_grad - delta)).astype(BF)
        dq = dot(score_grad, keys) * 0.125
        dq_ref[:, cols] = turn_back(dq, qcos_ref[...], qsin_ref[...]).astype(BF)
        dk_acc[...] += dot(score_grad, query, ((0,), (0,)))
        dv_acc[...] += dot(probs.astype(BF), grad, ((0,), (0,)))

    @pl.when(step == pl.num_programs(0) - 1)
    def _():
        dk = turn_back(dk_acc[...] * 0.125, kcos_ref[...], ksin_ref[...])
        dkv_ref[:, :HEAD_DIM] = dk.astype(BF)
        dkv_ref[:, HEAD_DIM:] = dv_acc[...].astype(BF)


def attend_back(queries, keys, values, qpos, kpos, out, lse, grad, cos, sin):
    length, wide = queries.shape
    rows = min(256, length)
    heads = wide // HEAD_DIM
    whole = lambda i: (0, 0)
    block = lambda i: (i, 0)
    return pl.pallas_call(
        backward_kernel,
        grid=(length // rows,),
        in_specs=[
            pl.BlockSpec((rows, wide), block),
            pl.BlockSpec((length, HEAD_DIM), whole),
            pl.BlockSpec((length, HEAD_DIM), whole),
            pl.BlockSpec((rows, 1), block),
            pl.BlockSpec((1, length), whole),
            pl.BlockSpec((rows, wide), block),
            pl.BlockSpec((rows, heads), block),
            pl.BlockSpec((rows, wide), block),
            pl.BlockSpec((rows, HEAD_DIM), block),
            pl.BlockSpec((rows, HEAD_DIM), block),
            pl.BlockSpec((length, HEAD_DIM), whole),
            pl.BlockSpec((length, HEAD_DIM), whole),
        ],
        out_specs=[
            pl.BlockSpec((rows, wide), block),
            pl.BlockSpec((length, 2 * HEAD_DIM), whole),
        ],
        out_shape=[
            jax.ShapeDtypeStruct((length, wide), BF),
            jax.ShapeDtypeStruct((length, 2 * HEAD_DIM), BF),
        ],
        scratch_shapes=[
            pltpu.VMEM((length, HEAD_DIM), F32),
            pltpu.VMEM((length, HEAD_DIM), F32),
        ],
        name="attend_back",
    )(queries, keys, values, qpos, kpos, out, lse, grad, cos, sin, cos, sin)


def turned_columns(weight):
    rows, wide = weight.shape
    halves = weight.reshape(rows, wide // HEAD_DIM, 2, HEAD_DIM // 2)
    return jnp.stack([-halves[:, :, 1], halves[:, :, 0]], axis=2).reshape(rows, wide)


def per_device(
    tokens,
    first_gain,
    query_weight,
    key_weight,
    value_weight,
    output_weight,
    second_gain,
    router_weight,
    expert_in,
    expert_out,
    chosen,
    out_grad,
):
    seqs, rows, width = tokens.shape
    ctx = lax.axis_size("ctx")
    fsdp = lax.axis_size("fsdp")
    c = lax.axis_index("ctx")
    s = lax.axis_index("fsdp")
    experts = router_weight.shape[1]
    local = expert_in.shape[1]
    length = ctx * rows
    slab = width // fsdp
    q_wide = HEADS * HEAD_DIM // ctx
    kv_shared = max(1, ctx // KV_HEADS)
    order = order_of(ctx)
    places = jnp.array(order, jnp.int32)

    def flip(value):
        return jnp.concatenate(
            [columns(value, ((s - j) % fsdp) * slab, slab) for j in range(fsdp)], axis=-1
        )

    def to_places(blocks):
        return jnp.stack([pick(blocks, c ^ place) for place in order], axis=0)

    own = flip(tokens[0])
    own_grad = flip(out_grad[0])
    named = jnp.sum(
        (chosen[0][..., None] == jnp.arange(experts, dtype=jnp.int32)).astype(F32), axis=1
    )
    flags = jnp.pad(named.astype(BF), ((0, 0), (0, 128 - experts)))
    shared_in = gather_ctx(jnp.concatenate([own, flags], axis=-1), ctx).reshape(length, -1)
    all_grad = gather_ctx(own_grad, ctx)
    all_x = shared_in[:, :width].astype(F32)
    all_named = shared_in[:, width : width + experts].astype(F32)

    kv_at = (c // kv_shared) * HEAD_DIM
    packed = jnp.concatenate(
        [
            columns(query_weight, c * q_wide, q_wide),
            columns(key_weight, kv_at, HEAD_DIM),
            columns(value_weight, kv_at, HEAD_DIM),
            router_weight,
            first_gain[:, None],
            second_gain[:, None],
            jnp.zeros((slab, 128 - experts - 2), BF),
        ],
        axis=-1,
    )
    packed = gather_fsdp(packed, fsdp)
    qkv_wide = q_wide + 2 * HEAD_DIM
    w_qkv = packed[:, :qkv_wide]
    w_router = packed[:, qkv_wide : qkv_wide + experts]
    gains = packed[:, qkv_wide + experts : qkv_wide + experts + 2].astype(F32).T
    gain_one = gains[:1]
    gain_two = gains[1:2]
    output_weight, expert_in, expert_out, packed = lax.optimization_barrier(
        (output_weight, expert_in, expert_out, packed)
    )
    w_output = gather_fsdp(output_weight, fsdp)
    w_in = gather_fsdp(expert_in.reshape(slab, -1), fsdp)
    w_out = gather_fsdp(expert_out.reshape(slab, -1), fsdp)

    block_index = c ^ places
    positions = (
        block_index[:, None] * rows + jnp.arange(rows, dtype=jnp.int32)[None, :]
    ).reshape(length)
    inverse = ROPE_BASE ** (-jnp.arange(HEAD_DIM // 2, dtype=F32) / (HEAD_DIM // 2))
    angles = positions.astype(F32)[:, None] * inverse[None, :]
    cos = jnp.tile(jnp.cos(angles), (1, 2))
    sin = jnp.tile(jnp.sin(angles), (1, 2))
    qpos = positions[:, None]
    kpos = positions[None, :]

    r_one = lax.rsqrt(jnp.mean(all_x * all_x, axis=-1, keepdims=True) + EPSILON)
    n_one = (all_x * r_one * gain_one).astype(BF)
    w_turned = turned_columns(w_qkv[:, : q_wide + HEAD_DIM])
    proj = dot(n_one, jnp.concatenate([w_qkv, w_turned], axis=-1))
    q_heads = q_wide // HEAD_DIM
    queries = (
        proj[:, :q_wide] * jnp.tile(cos, (1, q_heads))
        + proj[:, qkv_wide : qkv_wide + q_wide] * jnp.tile(sin, (1, q_heads))
    ).astype(BF)
    keys = (
        proj[:, q_wide : q_wide + HEAD_DIM] * cos + proj[:, qkv_wide + q_wide :] * sin
    ).astype(BF)
    values = proj[:, q_wide + HEAD_DIM : qkv_wide].astype(BF)
    heads_low, heads_high, lse = attend(queries, keys, values, qpos, kpos)

    sent = heads_low.reshape(ctx, rows, q_wide)
    at = [order.index(k) for k in range(ctx)]
    pieces = jnp.stack(exchange_ctx([sent[at[k]] for k in range(ctx)], ctx), axis=0)
    attended = flip(jnp.concatenate([pick(pieces, c ^ m) for m in range(ctx)], axis=-1))
    own_x = own.astype(F32)
    hidden = own_x + RESIDUAL * flip(dot(attended, w_output))
    r_two = lax.rsqrt(jnp.mean(hidden * hidden, axis=-1, keepdims=True) + EPSILON)
    n_two = (hidden * r_two * gain_two).astype(BF)
    all_two = gather_ctx(n_two, ctx)

    def gates(values_low, mask):
        logits = dot(values_low, w_router)
        return jax.nn.softmax(jnp.where(mask > 0, logits, -1e30), axis=-1) * mask

    all_gates = gates(all_two.reshape(length, width), all_named)
    loc_named = columns(all_named, c * local, local).reshape(ctx, rows, local)
    loc_gates = columns(all_gates, c * local, local).reshape(ctx, rows, local)
    before = (
        jnp.arange(rows, dtype=jnp.int32)[:, None] > jnp.arange(rows, dtype=jnp.int32)[None, :]
    ).astype(BF)
    rank = jnp.einsum(
        "tu,jue->jet", before, loc_named.astype(BF), preferred_element_type=F32
    )
    named_t = jnp.swapaxes(loc_named, 1, 2)
    gates_t = jnp.swapaxes(loc_gates, 1, 2)
    slots = jnp.arange(MOST, dtype=F32)[:, None]
    hit = (rank[:, :, None, :] == slots) & (named_t[:, :, None, :] > 0)
    chooser = hit.astype(BF)
    gate_rows = jnp.sum(jnp.where(hit, gates_t[:, :, None, :], 0.0), axis=-1)
    flat = (ctx * MOST, width)
    chunks_x = []
    chunks_gy = []
    for e in range(local):
        chunks_x.append(
            jnp.einsum("jqt,jtd->jqd", chooser[:, e], all_two, preferred_element_type=F32)
            .astype(BF)
            .reshape(flat)
        )
        chunks_gy.append(
            jnp.einsum("jqt,jtd->jqd", chooser[:, e], all_grad, preferred_element_type=F32)
            .reshape(flat)
        )
    moe = 0.0
    back = 0.0
    in_terms = []
    out_terms = []
    gate_terms = []
    for e in range(local):
        x_e = chunks_x[e]
        gy_e = chunks_gy[e]
        w_in_e = w_in[:, e * 2 * FF : (e + 1) * 2 * FF]
        w_out_e = w_out[:, e * FF : (e + 1) * FF]
        g_e = gate_rows[:, e].reshape(ctx * MOST, 1)
        u = dot(x_e, w_in_e)
        gate = u[:, :FF]
        up = u[:, FF:]
        sig = jax.nn.sigmoid(gate)
        swish = gate * sig
        act = (swish * up).astype(BF)
        dy = (RESIDUAL * g_e * gy_e).astype(BF)
        out_terms.append(dot(dy, act, ((0,), (0,))))
        dact = dot(dy, w_out_e)
        dgate = dact * up * (sig * (1.0 + gate * (1.0 - sig)))
        du = jnp.concatenate([dgate, dact * swish], axis=-1).astype(BF)
        in_terms.append(dot(x_e, du, ((0,), (0,))))
        y = dot(act, w_out_e, ((1,), (1,))).astype(BF).astype(F32)
        gate_terms.append(RESIDUAL * jnp.sum(gy_e * y, axis=-1).reshape(ctx, MOST))
        dn = dot(du, w_in_e, ((1,), (1,))).astype(BF).reshape(ctx, MOST, width)
        wy = (g_e * y).astype(BF).reshape(ctx, MOST, width)
        moe = moe + jnp.einsum("jqt,jqd->jtd", chooser[:, e], wy, preferred_element_type=F32)
        back = back + jnp.einsum("jqt,jqd->jtd", chooser[:, e], dn, preferred_element_type=F32)
    dg_slots = jnp.stack(gate_terms, axis=1)
    dg_loc = jnp.sum(jnp.where(hit, dg_slots[..., None], 0.0), axis=2)
    place = (
        jnp.arange(experts, dtype=jnp.int32)[None, :]
        == c * local + jnp.arange(local, dtype=jnp.int32)[:, None]
    ).astype(F32)
    dg_all = jnp.sum(jnp.swapaxes(dg_loc, 1, 2)[..., None] * place, axis=2)
    dg_high = dg_all.astype(BF)
    dg_rest = (dg_all - dg_high.astype(F32)).astype(BF)
    pad = jnp.zeros((ctx, rows, 128 - 2 * experts), BF)
    back = jnp.concatenate([back.astype(BF), dg_high, dg_rest, pad], axis=-1)
    back = scatter_ctx(back, ctx)
    in_grad = scatter_fsdp(jnp.concatenate(in_terms, axis=-1), fsdp).reshape(
        slab, local, 2 * FF
    )
    out_grad_w = scatter_fsdp(jnp.concatenate(out_terms, axis=-1), fsdp).reshape(
        slab, local, FF
    )
    layer_out = flip((hidden + RESIDUAL * scatter_ctx(moe.astype(BF), ctx)).astype(BF))

    dg = back[:, width : width + experts] + back[:, width + experts : width + 2 * experts]
    own_gates = gates(n_two, named)
    dlogits = (
        own_gates * (dg - jnp.sum(own_gates * dg, axis=-1, keepdims=True))
    ).astype(BF)
    dn_two = back[:, :width] + dot(dlogits, w_router, ((1,), (1,)))
    router_term = dot(n_two, dlogits, ((0,), (0,)))
    gain_two_term = jnp.sum(dn_two * hidden * r_two, axis=0)
    pulled = dn_two * gain_two
    dh = (
        own_grad.astype(F32)
        + r_two * pulled
        - hidden * r_two * r_two * r_two * jnp.mean(pulled * hidden, axis=-1, keepdims=True)
    )
    da = flip((RESIDUAL * dh).astype(BF))
    do_own = flip(dot(da, w_output, ((1,), (1,))).astype(BF))
    do_blocks = [columns(do_own, (c ^ k) * q_wide, q_wide) for k in range(ctx)]
    do_pieces = exchange_ctx(do_blocks, ctx)
    do_heads = jnp.concatenate([do_pieces[k] for k in order], axis=0)
    output_term = scatter_fsdp(dot(attended, da, ((0,), (0,))), fsdp)
    output_out = lax.psum(output_term.astype(BF), "ctx").astype(F32)

    dq, dkv = attend_back(
        queries, keys, values, qpos, kpos, heads_high, lse, do_heads, cos, sin
    )
    d_qkv = jnp.concatenate([dq, dkv], axis=-1)
    dn_one = dot(d_qkv, w_qkv, ((1,), (1,))).astype(BF).reshape(ctx, rows, width)
    dn_one = scatter_ctx(dn_one, ctx)
    w_term = dot(n_one, d_qkv, ((0,), (0,)))
    gain_one_term = jnp.sum(w_term * w_qkv.astype(F32), axis=-1, keepdims=True) / gain_one.T
    small = jnp.concatenate(
        [
            w_term,
            router_term,
            gain_one_term,
            gain_two_term[:, None],
            jnp.zeros((width, 128 - experts - 2), F32),
        ],
        axis=-1,
    )
    small = gather_ctx(scatter_fsdp(small, fsdp).astype(BF), ctx)
    where = jnp.array(at, jnp.int32)
    shards = [pick(small, where[c ^ m]).astype(F32) for m in range(ctx)]
    query_out = jnp.concatenate([shard[:, :q_wide] for shard in shards], axis=-1)
    key_parts = [shard[:, q_wide : q_wide + HEAD_DIM] for shard in shards]
    value_parts = [shard[:, q_wide + HEAD_DIM : qkv_wide] for shard in shards]
    key_out = jnp.concatenate(
        [sum(key_parts[i : i + kv_shared]) for i in range(0, ctx, kv_shared)], axis=-1
    )
    value_out = jnp.concatenate(
        [sum(value_parts[i : i + kv_shared]) for i in range(0, ctx, kv_shared)], axis=-1
    )
    rest = jnp.sum(small[:, :, qkv_wide:].astype(F32), axis=0)
    router_out = rest[:, :experts]
    gain_one_out = rest[:, experts]
    gain_two_out = rest[:, experts + 1]

    pulled_one = dn_one * gain_one
    own_r = lax.rsqrt(jnp.mean(own_x * own_x, axis=-1, keepdims=True) + EPSILON)
    tokens_grad = (
        dh
        + own_r * pulled_one
        - own_x * own_r * own_r * own_r
        * jnp.mean(pulled_one * own_x, axis=-1, keepdims=True)
    )
    tokens_grad = flip(tokens_grad)
    return (
        layer_out[None],
        tokens_grad[None],
        gain_one_out,
        query_out,
        key_out,
        value_out,
        output_out,
        gain_two_out,
        router_out,
        in_grad,
        out_grad_w,
    )


def solution(mesh):
    in_specs = (
        P("fsdp", "ctx", None),
        P("fsdp"),
        P("fsdp", None),
        P("fsdp", None),
        P("fsdp", None),
        P("fsdp", None),
        P("fsdp"),
        P("fsdp", None),
        P("fsdp", "ctx", None),
        P("fsdp", "ctx", None),
        P("fsdp", "ctx", None),
        P("fsdp", "ctx", None),
    )
    out_specs = (
        P("fsdp", "ctx", None),
        P("fsdp", "ctx", None),
        P("fsdp"),
        P("fsdp", None),
        P("fsdp", None),
        P("fsdp", None),
        P("fsdp", None),
        P("fsdp"),
        P("fsdp", None),
        P("fsdp", "ctx", None),
        P("fsdp", "ctx", None),
    )
    return jax.shard_map(
        per_device, mesh=mesh, in_specs=in_specs, out_specs=out_specs, check_vma=False
    )
```

time: 896 us -> 649 us (0.72)
  waiting for transfers between devices: 607 us -> 219 us
  blocking collectives: 118 us -> 0 us
  starting transfers between devices: 17.3 us -> 124 us
  local copies, waits for them, and re-layouts: 45.1 us -> 118 us
  other arithmetic: 20.8 us -> 68.8 us
  Pallas kernels: 0 us -> 18.3 us
  between operations: 15.6 us -> 32.1 us
    reduce_scatter x8 -> x0, waiting for transfers between devices: 290 us -> none  [the longest x1 72.4 us: per_device(): lax.psum_scatter(gate_up_term.astype(jnp.bfloat16), 'fsdp', scatter_dimen...]
    all_gather x8 -> x0, waiting for transfers between devices: 240 us -> none  [the longest x1 48.2 us: per_device(): lax.all_gather(expert_in, 'fsdp', axis=0, tiled=True)]
    ppermute x0 -> x85, waiting for transfers between devices: none -> 170 us  [the longest x32 123 us: shift_fsdp(): lax.ppermute(value, 'fsdp', [(i, (i + step) % size) for i in range(size)])]
    ppermute x0 -> x85, starting transfers between devices: none -> 124 us  [the longest x32 85.9 us: shift_fsdp(): lax.ppermute(value, 'fsdp', [(i, (i + step) % size) for i in range(size)])]
    all_to_all x2 -> x0, blocking collectives: 59.4 us -> none  [the longest x1 30.3 us: per_device(): lax.all_to_all(outgoing, 'ctx', split_axis=1, concat_axis=2, tiled=True)]
    all_gather x3 -> x0, blocking collectives: 35.3 us -> none  [the longest x1 13.1 us: per_device(): lax.all_gather(router_weight, 'fsdp', axis=0, tiled=True)]
    all_to_all x2 -> x0, waiting for transfers between devices: 29.1 us -> none  [the longest x1 15.8 us: per_device(): lax.all_to_all(row_grad, 'ctx', split_axis=2, concat_axis=1, tiled=True)]
    slice x0 -> x41, local copies, waits for them, and re-layouts: none -> 27.2 us  [the longest x4 4.57 us: scatter_ctx(): blocks = add_low(blocks[:half], swap_ctx(blocks[half:], 1, size))]
  transfers between devices with their start and end apart: 19 -> 86, of which waited for: 19 -> 36; matrix products, arithmetic and copies ran while one was open for 9% -> 26% of each run, Pallas kernels for 0% -> 3%
where the time goes in v1:
time: 649 us; the launch traced here: 640 us
  waiting for transfers between devices  219 us (34%)
  starting transfers between devices  124 us (19%)
  local copies, waits for them, and re-layouts  118 us (18%)
  other arithmetic  68.8 us (11%)
  matrix products  59.4 us (9%)
  between operations  32.1 us (5%)
  Pallas kernels  18.3 us (3%)
    ppermute x32, waiting for transfers between devices, shift_fsdp(): lax.ppermute(value, 'fsdp', [(i, (i + step) % size) for i in range(size)])  123 us
    ppermute x32, starting transfers between devices, shift_fsdp(): lax.ppermute(value, 'fsdp', [(i, (i + step) % size) for i in range(size)])  85.9 us
    psum x1, waiting for transfers between devices, per_device(): output_out = lax.psum(output_term.astype(BF), 'ctx').astype(F32)  48.8 us
    unnamed x310, local copies, waits for them, and re-layouts  48 us
    ppermute x53, waiting for transfers between devices, swap_ctx(): return lax.ppermute(value, 'ctx', [(i, i ^ bit) for i in range(size)])  46.7 us
    dot_general x22, matrix products, dot(): return lax.dot_general(a, b, (dims, ((), ())), preferred_element_type=F32)  43.4 us
    ppermute x53, starting transfers between devices, swap_ctx(): return lax.ppermute(value, 'ctx', [(i, i ^ bit) for i in range(size)])  38.5 us
    another operation x28, other arithmetic, gather_half(): value = jnp.stack([value, other], axis=axis)  19.3 us
  transfers between devices with their start and end apart: 86, of which 36 were waited for; matrix products, arithmetic and copies ran while one was open for 26% of the time, Pallas kernels for 3%

profile of v1, /device:TPU:0, one launch (start us, length us, event | category | flops | bytes accessed | tf_op | source)
XLA Modules:
  0.0 640.0 jit_solution(8992635320863085698)
XLA Ops:
  11.0 5.1 collective-permute-start.8
  58.7 4.6 collective-permute-done.7
  63.2 3.1 collective-permute-start.9
  73.4 4.3 collective-permute-start.33
  77.9 3.8 collective-permute-start.19
  83.6 9.8 %collective-permute-done.33 = bf16[256,1024]{1,0:T(8,128)(2,1)S(1)} collective-permute-done((bf16[256,1024]{1,0:T(8,128)(2,1)S(1)}, bf16[256,1024]{1,0:T(8,128)(2,1)S(1)}, u32[]{:S(2)}, u32[]{:S(2)}) %collective-permute-start.33) | collective-permute-done | bytes 524320 | tf_op jit(solution)/shard_map/ppermute | solution.py:105
  95.4 6.5 %collective-permute-done.31 = bf16[256,1024]{1,0:T(8,128)(2,1)S(1)} collective-permute-done((bf16[256,1024]{1,0:T(8,128)(2,1)S(1)}, bf16[256,1024]{1,0:T(8,128)(2,1)S(1)}, u32[]{:S(2)}, u32[]{:S(2)}) %collective-permute-start.31) | collective-permute-done | bytes 524320 | tf_op jit(solution)/shard_map/ppermute | solution.py:105
  104.6 8.0 %collective-permute-done.19 = bf16[256,1024]{1,0:T(8,128)(2,1)S(1)} collective-permute-done((bf16[256,1024]{1,0:T(8,128)(2,1)S(1)}, bf16[256,1024]{1,0:T(8,128)(2,1)S(1)}, u32[]{:S(2)}, u32[]{:S(2)}) %collective-permute-start.19) | collective-permute-done | bytes 524320 | tf_op jit(solution)/shard_map/ppermute | solution.py:105
  113.4 10.9 %collective-permute-done.17 = bf16[256,1024]{1,0:T(8,128)(2,1)S(1)} collective-permute-done((bf16[256,1024]{1,0:T(8,128)(2,1)S(1)}, bf16[256,1024]{1,0:T(8,128)(2,1)S(1)}, u32[]{:S(2)}, u32[]{:S(2)}) %collective-permute-start.17) | collective-permute-done | bytes 524320 | tf_op jit(solution)/shard_map/ppermute | solution.py:105
  136.7 16.6 %collective-permute-done.32 = bf16[128,1024]{1,0:T(8,128)(2,1)} collective-permute-done((bf16[128,1024]{1,0:T(8,128)(2,1)}, bf16[128,1024]{1,0:T(8,128)(2,1)}, u32[]{:S(2)}, u32[]{:S(2)}) %collective-permute-start.32) | collective-permute-done | bytes 262176 | tf_op jit(solution)/shard_map/ppermute | solution.py:105
  160.9 3.2 collective-permute-done.20
  198.8 7.3 %attend.1 = (bf16[1024,128]{1,0:T(8,128)(2,1)}, f32[1024,128]{1,0:T(8,128)}, f32[1024,2]{1,0:T(8,128)}) custom-call(bf16[1024,128]{1,0:T(8,128)(2,1)} %add_convert_fusion.9.q_ref, bf16[1024,64]{1,0:T(8,128)(2,1)} %add_convert_fusion.8.k_ref, bf16[1024,64]{1,0:T(8,128)(2,1)} %copy.314.v_ref, s32[1024,1]{1,0:T(8,128)} %copy.251.qpos_ref, s32[1,1024]{1,0:T(1,128)} %bitcast.449), custom_call_target="tpu_custom_call" | custom-call | tf_op jit(solution)/shard_map/attend/pallas_call | solution.py:174
  214.9 3.6 collective-permute-done.12
  218.5 3.9 collective-permute-done.13
  222.4 3.3 collective-permute-done.14
  236.8 20.2 %collective-permute-start.28 = (bf16[128,2048]{1,0:T(8,128)(2,1)S(1)}, bf16[128,2048]{1,0:T(8,128)(2,1)S(1)}, u32[]{:S(2)}, u32[]{:S(2)}) collective-permute-start(bf16[128,2048]{1,0:T(8,128)(2,1)S(1)} %slice.610), channel_id=1, source_target_pairs={{0,1},{1,2},{2,3},{3,0},{4,5},{5,6},{6,7},{7,4},{8,9},{9,10},{10,1... | collective-permute-start | bytes 1572872 | tf_op jit(solution)/shard_map/ppermute | solution.py:105
  261.6 2.8 collective-permute-done.22
  264.5 4.9 collective-permute-done.28
  269.4 9.5 %collective-permute-done.30 = bf16[128,2048]{1,0:T(8,128)(2,1)S(1)} collective-permute-done((bf16[128,2048]{1,0:T(8,128)(2,1)S(1)}, bf16[128,2048]{1,0:T(8,128)(2,1)S(1)}, u32[]{:S(2)}, u32[]{:S(2)}) %collective-permute-start.30) | collective-permute-done | bytes 524320 | tf_op jit(solution)/shard_map/ppermute | solution.py:105
  289.9 3.1 convolution_convert_fusion.1
  300.6 2.9 fusion.26
  308.2 3.3 fusion.30
  323.5 3.6 multiply_convert_fusion.3
  346.0 4.3 collective-permute-start.83
  350.2 2.8 fusion.97
  361.2 3.8 collective-permute-start.79
  365.0 3.1 add_convert_fusion
  369.6 3.8 collective-permute-start.84
  378.4 8.9 %collective-permute-done.79 = bf16[128,2048]{0,1:T(8,128)(2,1)S(1)} collective-permute-done((bf16[128,2048]{0,1:T(8,128)(2,1)S(1)}, bf16[128,2048]{0,1:T(8,128)(2,1)S(1)}, u32[]{:S(2)}, u32[]{:S(2)}) %collective-permute-start.79) | collective-permute-done | bytes 524320 | tf_op jit(solution)/shard_map/ppermute | solution.py:105
  390.2 10.1 %collective-permute-done.82 = bf16[256,1024]{0,1:T(8,128)(2,1)S(1)} collective-permute-done((bf16[256,1024]{0,1:T(8,128)(2,1)S(1)}, bf16[256,1024]{0,1:T(8,128)(2,1)S(1)}, u32[]{:S(2)}, u32[]{:S(2)}) %collective-permute-start.82) | collective-permute-done | bytes 524320 | tf_op jit(solution)/shard_map/ppermute | solution.py:105
  400.3 11.4 %collective-permute-start.80 = (bf16[256,2048]{0,1:T(8,128)(2,1)}, bf16[256,2048]{0,1:T(8,128)(2,1)}, u32[]{:S(2)}, u32[]{:S(2)}) collective-permute-start(bf16[256,2048]{0,1:T(8,128)(2,1)} %get-tuple-element.108), channel_id=1, source_target_pairs={{0,3},{1,0},{2,1},{3,2},{4,7},{5,4},{6,5},{7,6},{8,11},{9,8},{10,9... | collective-permute-start | bytes 3145736 | tf_op jit(solution)/shard_map/ppermute | solution.py:105
  412.9 2.8 copy.296
  422.6 3.8 collective-permute-done.38
  428.8 4.1 collective-permute-done.47
  440.4 13.9 %collective-permute-done.80 = bf16[256,2048]{0,1:T(8,128)(2,1)} collective-permute-done((bf16[256,2048]{0,1:T(8,128)(2,1)}, bf16[256,2048]{0,1:T(8,128)(2,1)}, u32[]{:S(2)}, u32[]{:S(2)}) %collective-permute-start.80) | collective-permute-done | bytes 1048608 | tf_op jit(solution)/shard_map/ppermute | solution.py:105
  465.6 2.7 fusion.174
  474.0 3.6 collective-permute-done.52
  478.3 4.1 collective-permute-done.53
  483.5 2.8 collective-permute-start.75
  487.1 11.0 %attend_back.1 = (bf16[1024,128]{1,0:T(8,128)(2,1)}, bf16[1024,128]{1,0:T(8,128)(2,1)}) custom-call(bf16[1024,128]{1,0:T(8,128)(2,1)} %add_convert_fusion.9.q_ref, bf16[1024,64]{1,0:T(8,128)(2,1)} %add_convert_fusion.8.k_ref, bf16[1024,64]{1,0:T(8,128)(2,1)} %copy.314.v_ref, s32[1024,1]{1,0:T(8,128)} %copy.251.qpos_ref, s32[1,1024]{1,0:T(1,128)} %bitcast.450, ...), custom_call_target="tpu_custom_call" | custom-call | tf_op jit(solution)/shard_map/attend_back/pallas_call | solution.py:245
  500.2 3.0 multiply_reduce_fusion
  506.2 3.8 collective-permute-start.65
  513.6 4.0 collective-permute-start.66
  519.6 4.0 collective-permute-start.76
  527.4 2.9 collective-permute-done.70
  535.5 3.4 collective-permute-done.74
  538.9 8.7 %collective-permute-done.76 = bf16[256,1024]{1,0:T(8,128)(2,1)S(1)} collective-permute-done((bf16[256,1024]{1,0:T(8,128)(2,1)S(1)}, bf16[256,1024]{1,0:T(8,128)(2,1)S(1)}, u32[]{:S(2)}, u32[]{:S(2)}) %collective-permute-start.76) | collective-permute-done | bytes 524320 | tf_op jit(solution)/shard_map/ppermute | solution.py:105
  554.6 48.8 %all-reduce.11.cloned.1.call-done = bf16[256,1024]{1,0:T(8,128)(2,1)} async-done(((bf16[256,1024]{1,0:T(8,128)(2,1)}), bf16[256,1024]{1,0:T(8,128)(2,1)}) %all-reduce.11.cloned.1.call-update) | async-done | bytes 524304 | tf_op jit(solution)/shard_map/psum | solution.py:495
  (691 shorter events, 288.3 us)
Async XLA Ops:
  7.2 596.2 %all-reduce.11.cloned.1.call-start = ((), (), s32[]{:S(2)}) async-start(), calls=%async_computation | async-start | bytes 1048576 | tf_op jit(solution)/shard_map/psum | solution.py:495
  11.0 45.8 %collective-permute-start.8 = (bf16[256,384]{0,1:T(8,128)(2,1)S(1)}, bf16[256,384]{0,1:T(8,128)(2,1)}, u32[]{:S(2)}, u32[]{:S(2)}) collective-permute-start(bf16[256,384]{0,1:T(8,128)(2,1)S(1)} %concatenate.173), channel_id=1, source_target_pairs={{0,3},{1,0},{2,1},{3,2},{4,7},{5,4},{6,5},{7,6},{8,11},{9,8},{10,9... | collective-permute-start | bytes 589832 | tf_op jit(solution)/shard_map/ppermute | solution.py:105
  16.1 38.1 %collective-permute-start.6 = (bf16[256,384]{0,1:T(8,128)(2,1)S(1)}, bf16[256,384]{0,1:T(8,128)(2,1)}, u32[]{:S(2)}, u32[]{:S(2)}) collective-permute-start(bf16[256,384]{0,1:T(8,128)(2,1)S(1)} %concatenate.173), channel_id=1, source_target_pairs={{0,1},{1,2},{2,3},{3,0},{4,5},{5,6},{6,7},{7,4},{8,9},{9,10},{10,1... | collective-permute-start | bytes 589832 | tf_op jit(solution)/shard_map/ppermute | solution.py:105
  18.1 32.3 %collective-permute-start = (bf16[128,512]{0,1:T(8,128)(2,1)}, bf16[128,512]{0,1:T(8,128)(2,1)}, u32[]{:S(2)}, u32[]{:S(2)}) collective-permute-start(bf16[128,512]{0,1:T(8,128)(2,1)} %get-tuple-element.256), channel_id=1, source_target_pairs={{0,16},{4,20},{8,24},{12,28},{16,0},{20,4},{24,8},{28,12},{1,17},{... | collective-permute-start | bytes 393224 | tf_op jit(solution)/shard_map/ppermute | solution.py:41
  20.7 27.3 %collective-permute-start.43 = (bf16[128,512]{0,1:T(8,128)(2,1)}, bf16[128,512]{0,1:T(8,128)(2,1)}, u32[]{:S(2)}, u32[]{:S(2)}) collective-permute-start(bf16[128,512]{0,1:T(8,128)(2,1)} %get-tuple-element.254), channel_id=1, source_target_pairs={{0,8},{4,12},{8,0},{12,4},{16,24},{20,28},{24,16},{28,20},{1,9},{5... | collective-permute-start | bytes 393224 | tf_op jit(solution)/shard_map/ppermute | solution.py:41
  23.1 23.2 %collective-permute-start.40 = (bf16[128,512]{0,1:T(8,128)(2,1)S(1)}, bf16[128,512]{0,1:T(8,128)(2,1)S(1)}, u32[]{:S(2)}, u32[]{:S(2)}) collective-permute-start(bf16[128,512]{0,1:T(8,128)(2,1)S(1)} %get-tuple-element.252), channel_id=1, source_target_pairs={{0,16},{4,20},{8,24},{12,28},{16,0},{20,4},{24,8},{28,12},{1,17},{... | collective-permute-start | bytes 393224 | tf_op jit(solution)/shard_map/ppermute | solution.py:41
  48.0 29.8 %collective-permute-start.41 = (bf16[2,128,512]{1,2,0:T(8,128)(2,1)S(1)}, bf16[2,128,512]{1,2,0:T(8,128)(2,1)S(1)}, u32[]{:S(2)}, u32[]{:S(2)}) collective-permute-start(bf16[2,128,512]{1,2,0:T(8,128)(2,1)S(1)} %get-tuple-element.209), channel_id=1, source_target_pairs={{0,8},{4,12},{8,0},{12,4},{16,24},{20,28},{24,16},{28,20},{1,9},{5... | collective-permute-start | bytes 786440 | tf_op jit(solution)/shard_map/ppermute | solution.py:41
  50.5 27.4 %collective-permute-start.44 = (bf16[2,128,512]{1,2,0:T(8,128)(2,1)S(1)}, bf16[2,128,512]{1,2,0:T(8,128)(2,1)S(1)}, u32[]{:S(2)}, u32[]{:S(2)}) collective-permute-start(bf16[2,128,512]{1,2,0:T(8,128)(2,1)S(1)} %get-tuple-element.215), channel_id=1, source_target_pairs={{0,16},{4,20},{8,24},{12,28},{16,0},{20,4},{24,8},{28,12},{1,17},{... | collective-permute-start | bytes 786440 | tf_op jit(solution)/shard_map/ppermute | solution.py:41
  53.7 28.1 %collective-permute-start.1 = (bf16[2,128,512]{1,2,0:T(8,128)(2,1)S(1)}, bf16[2,128,512]{1,2,0:T(8,128)(2,1)S(1)}, u32[]{:S(2)}, u32[]{:S(2)}) collective-permute-start(bf16[2,128,512]{1,2,0:T(8,128)(2,1)S(1)} %get-tuple-element.236), channel_id=1, source_target_pairs={{0,8},{4,12},{8,0},{12,4},{16,24},{20,28},{24,16},{28,20},{1,9},{5... | collective-permute-start | bytes 786440 | tf_op jit(solution)/shard_map/ppermute | solution.py:41
  54.2 29.2 %collective-permute-start.4 = (bf16[2,128,640]{1,2,0:T(8,128)(2,1)S(1)}, bf16[2,128,640]{1,2,0:T(8,128)(2,1)S(1)}, u32[]{:S(2)}, u32[]{:S(2)}) collective-permute-start(bf16[2,128,640]{1,2,0:T(8,128)(2,1)S(1)} %get-tuple-element.183), channel_id=1, source_target_pairs={{0,16},{4,20},{8,24},{12,28},{16,0},{20,4},{24,8},{28,12},{1,17},{... | collective-permute-start | bytes 983048 | tf_op jit(solution)/shard_map/ppermute | solution.py:41
  73.4 19.9 %collective-permute-start.33 = (bf16[256,1024]{1,0:T(8,128)(2,1)S(1)}, bf16[256,1024]{1,0:T(8,128)(2,1)S(1)}, u32[]{:S(2)}, u32[]{:S(2)}) collective-permute-start(bf16[256,1024]{1,0:T(8,128)(2,1)S(1)} %bitcast.384), channel_id=1, source_target_pairs={{0,3},{1,0},{2,1},{3,2},{4,7},{5,4},{6,5},{7,6},{8,11},{9,8},{10,9... | collective-permute-start | bytes 1572872 | tf_op jit(solution)/shard_map/ppermute | solution.py:105
  77.8 24.0 %collective-permute-start.31 = (bf16[256,1024]{1,0:T(8,128)(2,1)S(1)}, bf16[256,1024]{1,0:T(8,128)(2,1)S(1)}, u32[]{:S(2)}, u32[]{:S(2)}) collective-permute-start(bf16[256,1024]{1,0:T(8,128)(2,1)S(1)} %bitcast.386), channel_id=1, source_target_pairs={{0,1},{1,2},{2,3},{3,0},{4,5},{5,6},{6,7},{7,4},{8,9},{9,10},{10,1... | collective-permute-start | bytes 1572872 | tf_op jit(solution)/shard_map/ppermute | solution.py:105
  77.9 34.7 %collective-permute-start.19 = (bf16[256,1024]{1,0:T(8,128)(2,1)S(1)}, bf16[256,1024]{1,0:T(8,128)(2,1)S(1)}, u32[]{:S(2)}, u32[]{:S(2)}) collective-permute-start(bf16[256,1024]{1,0:T(8,128)(2,1)S(1)} %copy-done.88), channel_id=1, source_target_pairs={{0,3},{1,0},{2,1},{3,2},{4,7},{5,4},{6,5},{7,6},{8,11},{9,8},{10,9... | collective-permute-start | bytes 1572872 | tf_op jit(solution)/shard_map/ppermute | solution.py:105
  81.7 42.5 %collective-permute-start.17 = (bf16[256,1024]{1,0:T(8,128)(2,1)S(1)}, bf16[256,1024]{1,0:T(8,128)(2,1)S(1)}, u32[]{:S(2)}, u32[]{:S(2)}) collective-permute-start(bf16[256,1024]{1,0:T(8,128)(2,1)S(1)} %copy-done.88), channel_id=1, source_target_pairs={{0,1},{1,2},{2,3},{3,0},{4,5},{5,6},{6,7},{7,4},{8,9},{9,10},{10,1... | collective-permute-start | bytes 1572872 | tf_op jit(solution)/shard_map/ppermute | solution.py:105
  83.4 41.7 %collective-permute-start.42 = (bf16[2,2,128,512]{2,3,0,1:T(8,128)(2,1)S(1)}, bf16[2,2,128,512]{2,3,0,1:T(8,128)(2,1)S(1)}, u32[]{:S(2)}, u32[]{:S(2)}) collective-permute-start(bf16[2,2,128,512]{2,3,0,1:T(8,128)(2,1)S(1)} %get-tuple-element.151), channel_id=1, source_target_pairs={{0,4},{4,0},{8,12},{12,8},{16,20},{20,16},{24,28},{28,24},{1,5},{5... | collective-permute-start | bytes 1572872 | tf_op jit(solution)/shard_map/ppermute | solution.py:41
  93.3 32.3 %collective-permute-start.45 = (bf16[2,2,128,512]{2,3,1,0:T(8,128)(2,1)S(1)}, bf16[2,2,128,512]{2,3,1,0:T(8,128)(2,1)S(1)}, u32[]{:S(2)}, u32[]{:S(2)}) collective-permute-start(bf16[2,2,128,512]{2,3,1,0:T(8,128)(2,1)S(1)} %get-tuple-element.153), channel_id=1, source_target_pairs={{0,4},{4,0},{8,12},{12,8},{16,20},{20,16},{24,28},{28,24},{1,5},{5... | collective-permute-start | bytes 1572872 | tf_op jit(solution)/shard_map/ppermute | solution.py:41
  101.8 156.4 %collective-permute-start.29 = (bf16[256,2048]{1,0:T(8,128)(2,1)}, bf16[256,2048]{1,0:T(8,128)(2,1)}, u32[]{:S(2)}, u32[]{:S(2)}) collective-permute-start(bf16[256,2048]{1,0:T(8,128)(2,1)} %bitcast.203), channel_id=1, source_target_pairs={{0,3},{1,0},{2,1},{3,2},{4,7},{5,4},{6,5},{7,6},{8,11},{9,8},{10,9... | collective-permute-start | bytes 3145736 | tf_op jit(solution)/shard_map/ppermute | solution.py:105
  124.2 42.2 %collective-permute-start.5 = (bf16[2,2,128,640]{2,3,1,0:T(8,128)(2,1)}, bf16[2,2,128,640]{2,3,1,0:T(8,128)(2,1)}, u32[]{:S(2)}, u32[]{:S(2)}) collective-permute-start(bf16[2,2,128,640]{2,3,1,0:T(8,128)(2,1)} %get-tuple-element.142), channel_id=1, source_target_pairs={{0,4},{4,0},{8,12},{12,8},{16,20},{20,16},{24,28},{28,24},{1,5},{5... | collective-permute-start | bytes 1966088 | tf_op jit(solution)/shard_map/ppermute | solution.py:41
  125.1 29.8 %collective-permute-start.34 = (bf16[128,1024]{1,0:T(8,128)(2,1)}, bf16[128,1024]{1,0:T(8,128)(2,1)}, u32[]{:S(2)}, u32[]{:S(2)}) collective-permute-start(bf16[128,1024]{1,0:T(8,128)(2,1)} %slice.616), channel_id=1, source_target_pairs={{0,3},{1,0},{2,1},{3,2},{4,7},{5,4},{6,5},{7,6},{8,11},{9,8},{10,9... | collective-permute-start | bytes 786440 | tf_op jit(solution)/shard_map/ppermute | solution.py:105
  125.6 27.6 %collective-permute-start.32 = (bf16[128,1024]{1,0:T(8,128)(2,1)}, bf16[128,1024]{1,0:T(8,128)(2,1)}, u32[]{:S(2)}, u32[]{:S(2)}) collective-permute-start(bf16[128,1024]{1,0:T(8,128)(2,1)} %slice.615), channel_id=1, source_target_pairs={{0,1},{1,2},{2,3},{3,0},{4,5},{5,6},{6,7},{7,4},{8,9},{9,10},{10,1... | collective-permute-start | bytes 786440 | tf_op jit(solution)/shard_map/ppermute | solution.py:105
  128.5 30.7 %collective-permute-start.18 = (bf16[128,1024]{1,0:T(8,128)(2,1)}, bf16[128,1024]{1,0:T(8,128)(2,1)}, u32[]{:S(2)}, u32[]{:S(2)}) collective-permute-start(bf16[128,1024]{1,0:T(8,128)(2,1)} %slice.601), channel_id=1, source_target_pairs={{0,1},{1,2},{2,3},{3,0},{4,5},{5,6},{6,7},{7,4},{8,9},{9,10},{10,1... | collective-permute-start | bytes 786440 | tf_op jit(solution)/shard_map/ppermute | solution.py:105
  154.9 80.8 %collective-permute-start.27 = (bf16[256,2048]{1,0:T(8,128)(2,1)}, bf16[256,2048]{1,0:T(8,128)(2,1)}, u32[]{:S(2)}, u32[]{:S(2)}) collective-permute-start(bf16[256,2048]{1,0:T(8,128)(2,1)} %bitcast.203), channel_id=1, source_target_pairs={{0,1},{1,2},{2,3},{3,0},{4,5},{5,6},{6,7},{7,4},{8,9},{9,10},{10,1... | collective-permute-start | bytes 3145736 | tf_op jit(solution)/shard_map/ppermute | solution.py:105
  207.9 17.8 %collective-permute-start.16 = (bf16[128,128]{1,0:T(8,128)(2,1)S(1)}, bf16[128,128]{1,0:T(8,128)(2,1)S(1)}, u32[]{:S(2)}, u32[]{:S(2)}) collective-permute-start(bf16[128,128]{1,0:T(8,128)(2,1)S(1)} %get-tuple-element.228), channel_id=1, source_target_pairs={{0,28},{4,24},{8,20},{12,16},{16,12},{20,8},{24,4},{28,0},{1,29},{... | collective-permute-start | bytes 98312 | tf_op jit(solution)/shard_map/ppermute | solution.py:41
  231.1 26.0 %collective-permute-start.21 = (bf16[128,512]{0,1:T(8,128)(2,1)S(1)}, bf16[128,512]{0,1:T(8,128)(2,1)S(1)}, u32[]{:S(2)}, u32[]{:S(2)}) collective-permute-start(bf16[128,512]{0,1:T(8,128)(2,1)S(1)} %get-tuple-element.221), channel_id=1, source_target_pairs={{0,16},{4,20},{8,24},{12,28},{16,0},{20,4},{24,8},{28,12},{1,17},{... | collective-permute-start | bytes 393224 | tf_op jit(solution)/shard_map/ppermute | solution.py:41
  234.8 25.9 %collective-permute-start.25 = (bf16[2,128,512]{1,2,0:T(8,128)(2,1)S(1)}, bf16[2,128,512]{1,2,0:T(8,128)(2,1)S(1)}, u32[]{:S(2)}, u32[]{:S(2)}) collective-permute-start(bf16[2,128,512]{1,2,0:T(8,128)(2,1)S(1)} %get-tuple-element.223), channel_id=1, source_target_pairs={{0,16},{4,20},{8,24},{12,28},{16,0},{20,4},{24,8},{28,12},{1,17},{... | collective-permute-start | bytes 786440 | tf_op jit(solution)/shard_map/ppermute | solution.py:41
  236.8 32.5 %collective-permute-start.28 = (bf16[128,2048]{1,0:T(8,128)(2,1)S(1)}, bf16[128,2048]{1,0:T(8,128)(2,1)S(1)}, u32[]{:S(2)}, u32[]{:S(2)}) collective-permute-start(bf16[128,2048]{1,0:T(8,128)(2,1)S(1)} %slice.610), channel_id=1, source_target_pairs={{0,1},{1,2},{2,3},{3,0},{4,5},{5,6},{6,7},{7,4},{8,9},{9,10},{10,1... | collective-permute-start | bytes 1572872 | tf_op jit(solution)/shard_map/ppermute | solution.py:105
  259.3 19.6 %collective-permute-start.30 = (bf16[128,2048]{1,0:T(8,128)(2,1)S(1)}, bf16[128,2048]{1,0:T(8,128)(2,1)S(1)}, u32[]{:S(2)}, u32[]{:S(2)}) collective-permute-start(bf16[128,2048]{1,0:T(8,128)(2,1)S(1)} %slice.611), channel_id=1, source_target_pairs={{0,3},{1,0},{2,1},{3,2},{4,7},{5,4},{6,5},{7,6},{8,11},{9,8},{10,9... | collective-permute-start | bytes 1572872 | tf_op jit(solution)/shard_map/ppermute | solution.py:105
  261.6 23.9 %collective-permute-start.26 = (bf16[2,2,128,512]{2,3,1,0:T(8,128)(2,1)}, bf16[2,2,128,512]{2,3,1,0:T(8,128)(2,1)}, u32[]{:S(2)}, u32[]{:S(2)}) collective-permute-start(bf16[2,2,128,512]{2,3,1,0:T(8,128)(2,1)} %get-tuple-element.157), channel_id=1, source_target_pairs={{0,4},{4,0},{8,12},{12,8},{16,20},{20,16},{24,28},{28,24},{1,5},{5... | collective-permute-start | bytes 1572872 | tf_op jit(solution)/shard_map/ppermute | solution.py:41
  346.0 22.2 %collective-permute-start.81 = (bf16[128,1024]{0,1:T(8,128)(2,1)}, bf16[128,1024]{0,1:T(8,128)(2,1)}, u32[]{:S(2)}, u32[]{:S(2)}) collective-permute-start(bf16[128,1024]{0,1:T(8,128)(2,1)} %get-tuple-element.119), channel_id=1, source_target_pairs={{0,1},{1,2},{2,3},{3,0},{4,5},{5,6},{6,7},{7,4},{8,9},{9,10},{10,1... | collective-permute-start | bytes 786440 | tf_op jit(solution)/shard_map/ppermute | solution.py:105
  346.0 22.2 %collective-permute-start.83 = (bf16[128,1024]{0,1:T(8,128)(2,1)}, bf16[128,1024]{0,1:T(8,128)(2,1)}, u32[]{:S(2)}, u32[]{:S(2)}) collective-permute-start(bf16[128,1024]{0,1:T(8,128)(2,1)} %get-tuple-element.120), channel_id=1, source_target_pairs={{0,3},{1,0},{2,1},{3,2},{4,7},{5,4},{6,5},{7,6},{8,11},{9,8},{10,9... | collective-permute-start | bytes 786440 | tf_op jit(solution)/shard_map/ppermute | solution.py:105
  357.1 58.6 %collective-permute-start.35 = (bf16[4,128,1024]{1,2,0:T(8,128)(2,1)}, bf16[4,128,1024]{1,2,0:T(8,128)(2,1)}, u32[]{:S(2)}, u32[]{:S(2)}) collective-permute-start(bf16[4,128,1024]{1,2,0:T(8,128)(2,1)} %slice.625), channel_id=1, source_target_pairs={{0,4},{4,0},{8,12},{12,8},{16,20},{20,16},{24,28},{28,24},{1,5},{5... | collective-permute-start | bytes 3145736 | tf_op jit(solution)/shard_map/ppermute | solution.py:41
  361.2 26.1 %collective-permute-start.79 = (bf16[128,2048]{0,1:T(8,128)(2,1)S(1)}, bf16[128,2048]{0,1:T(8,128)(2,1)S(1)}, u32[]{:S(2)}, u32[]{:S(2)}) collective-permute-start(bf16[128,2048]{0,1:T(8,128)(2,1)S(1)} %get-tuple-element.112), channel_id=1, source_target_pairs={{0,3},{1,0},{2,1},{3,2},{4,7},{5,4},{6,5},{7,6},{8,11},{9,8},{10,9... | collective-permute-start | bytes 1572872 | tf_op jit(solution)/shard_map/ppermute | solution.py:105
  369.5 30.8 %collective-permute-start.82 = (bf16[256,1024]{0,1:T(8,128)(2,1)S(1)}, bf16[256,1024]{0,1:T(8,128)(2,1)S(1)}, u32[]{:S(2)}, u32[]{:S(2)}) collective-permute-start(bf16[256,1024]{0,1:T(8,128)(2,1)S(1)} %get-tuple-element.109), channel_id=1, source_target_pairs={{0,1},{1,2},{2,3},{3,0},{4,5},{5,6},{6,7},{7,4},{8,9},{9,10},{10,1... | collective-permute-start | bytes 1572872 | tf_op jit(solution)/shard_map/ppermute | solution.py:105
  369.6 42.2 %collective-permute-start.84 = (bf16[256,1024]{0,1:T(8,128)(2,1)S(1)}, bf16[256,1024]{0,1:T(8,128)(2,1)S(1)}, u32[]{:S(2)}, u32[]{:S(2)}) collective-permute-start(bf16[256,1024]{0,1:T(8,128)(2,1)S(1)} %get-tuple-element.110), channel_id=1, source_target_pairs={{0,3},{1,0},{2,1},{3,2},{4,7},{5,4},{6,5},{7,6},{8,11},{9,8},{10,9... | collective-permute-start | bytes 1572872 | tf_op jit(solution)/shard_map/ppermute | solution.py:105
  377.8 41.2 %collective-permute-start.46 = (bf16[4,128,1152]{1,2,0:T(8,128)(2,1)}, bf16[4,128,1152]{1,2,0:T(8,128)(2,1)}, u32[]{:S(2)}, u32[]{:S(2)}) collective-permute-start(bf16[4,128,1152]{1,2,0:T(8,128)(2,1)} %slice.636), channel_id=1, source_target_pairs={{0,4},{4,0},{8,12},{12,8},{16,20},{20,16},{24,28},{28,24},{1,5},{5... | collective-permute-start | bytes 3538952 | tf_op jit(solution)/shard_map/ppermute | solution.py:41
  389.2 51.2 %collective-permute-start.78 = (bf16[256,2048]{0,1:T(8,128)(2,1)}, bf16[256,2048]{0,1:T(8,128)(2,1)}, u32[]{:S(2)}, u32[]{:S(2)}) collective-permute-start(bf16[256,2048]{0,1:T(8,128)(2,1)} %get-tuple-element.107), channel_id=1, source_target_pairs={{0,1},{1,2},{2,3},{3,0},{4,5},{5,6},{6,7},{7,4},{8,9},{9,10},{10,1... | collective-permute-start | bytes 3145736 | tf_op jit(solution)/shard_map/ppermute | solution.py:105
  400.3 54.0 %collective-permute-start.80 = (bf16[256,2048]{0,1:T(8,128)(2,1)}, bf16[256,2048]{0,1:T(8,128)(2,1)}, u32[]{:S(2)}, u32[]{:S(2)}) collective-permute-start(bf16[256,2048]{0,1:T(8,128)(2,1)} %get-tuple-element.108), channel_id=1, source_target_pairs={{0,3},{1,0},{2,1},{3,2},{4,7},{5,4},{6,5},{7,6},{8,11},{9,8},{10,9... | collective-permute-start | bytes 3145736 | tf_op jit(solution)/shard_map/ppermute | solution.py:105
  420.8 17.7 %collective-permute-start.49 = (bf16[2,128,640]{1,2,0:T(8,128)(2,1)S(1)}, bf16[2,128,640]{1,2,0:T(8,128)(2,1)S(1)}, u32[]{:S(2)}, u32[]{:S(2)}) collective-permute-start(bf16[2,128,640]{1,2,0:T(8,128)(2,1)S(1)} %slice.643), channel_id=1, source_target_pairs={{0,16},{4,20},{8,24},{12,28},{16,0},{20,4},{24,8},{28,12},{1,17},{... | collective-permute-start | bytes 983048 | tf_op jit(solution)/shard_map/ppermute | solution.py:41
  434.3 24.5 %collective-permute-start.48 = (bf16[128,512]{0,1:T(8,128)(2,1)S(1)}, bf16[128,512]{0,1:T(8,128)(2,1)}, u32[]{:S(2)}, u32[]{:S(2)}) collective-permute-start(bf16[128,512]{0,1:T(8,128)(2,1)S(1)} %slice_bitcast_fusion.14), channel_id=1, source_target_pairs={{0,16},{4,20},{8,24},{12,28},{16,0},{20,4},{24,8},{28,12},{1,17},{... | collective-permute-start | bytes 393224 | tf_op jit(solution)/shard_map/ppermute | solution.py:41
  439.3 20.5 %collective-permute-start.50 = (bf16[128,640]{0,1:T(8,128)(2,1)}, bf16[128,640]{0,1:T(8,128)(2,1)}, u32[]{:S(2)}, u32[]{:S(2)}) collective-permute-start(bf16[128,640]{0,1:T(8,128)(2,1)} %slice_bitcast_fusion.8), channel_id=1, source_target_pairs={{0,8},{4,12},{8,0},{12,4},{16,24},{20,28},{24,16},{28,20},{1,9},{5... | collective-permute-start | bytes 491528 | tf_op jit(solution)/shard_map/ppermute | solution.py:41
  482.4 35.2 %collective-permute-start.73 = (bf16[128,1024]{1,0:T(8,128)(2,1)}, bf16[128,1024]{1,0:T(8,128)(2,1)S(1)}, u32[]{:S(2)}, u32[]{:S(2)}) collective-permute-start(bf16[128,1024]{1,0:T(8,128)(2,1)} %get-tuple-element.121), channel_id=1, source_target_pairs={{0,1},{1,2},{2,3},{3,0},{4,5},{5,6},{6,7},{7,4},{8,9},{9,10},{10,1... | collective-permute-start | bytes 786440 | tf_op jit(solution)/shard_map/ppermute | solution.py:105
  483.5 34.1 %collective-permute-start.75 = (bf16[128,1024]{1,0:T(8,128)(2,1)}, bf16[128,1024]{1,0:T(8,128)(2,1)}, u32[]{:S(2)}, u32[]{:S(2)}) collective-permute-start(bf16[128,1024]{1,0:T(8,128)(2,1)} %get-tuple-element.122), channel_id=1, source_target_pairs={{0,3},{1,0},{2,1},{3,2},{4,7},{5,4},{6,5},{7,6},{8,11},{9,8},{10,9... | collective-permute-start | bytes 786440 | tf_op jit(solution)/shard_map/ppermute | solution.py:105
  512.4 93.1 %collective-permute-start.58 = (bf16[4,128,1024]{1,2,0:T(8,128)(2,1)}, bf16[4,128,1024]{1,2,0:T(8,128)(2,1)}, u32[]{:S(2)}, u32[]{:S(2)}) collective-permute-start(bf16[4,128,1024]{1,2,0:T(8,128)(2,1)} %copy.287), channel_id=1, source_target_pairs={{0,4},{4,0},{8,12},{12,8},{16,20},{20,16},{24,28},{28,24},{1,5},{5... | collective-permute-start | bytes 3145736 | tf_op jit(solution)/shard_map/ppermute | solution.py:41
  519.5 19.4 %collective-permute-start.74 = (bf16[256,1024]{1,0:T(8,128)(2,1)S(1)}, bf16[256,1024]{1,0:T(8,128)(2,1)S(1)}, u32[]{:S(2)}, u32[]{:S(2)}) collective-permute-start(bf16[256,1024]{1,0:T(8,128)(2,1)S(1)} %get-tuple-element.113), channel_id=1, source_target_pairs={{0,1},{1,2},{2,3},{3,0},{4,5},{5,6},{6,7},{7,4},{8,9},{9,10},{10,1... | collective-permute-start | bytes 1572872 | tf_op jit(solution)/shard_map/ppermute | solution.py:105
  519.6 28.0 %collective-permute-start.76 = (bf16[256,1024]{1,0:T(8,128)(2,1)S(1)}, bf16[256,1024]{1,0:T(8,128)(2,1)S(1)}, u32[]{:S(2)}, u32[]{:S(2)}) collective-permute-start(bf16[256,1024]{1,0:T(8,128)(2,1)S(1)} %get-tuple-element.114), channel_id=1, source_target_pairs={{0,3},{1,0},{2,1},{3,2},{4,7},{5,4},{6,5},{7,6},{8,11},{9,8},{10,9... | collective-permute-start | bytes 1572872 | tf_op jit(solution)/shard_map/ppermute | solution.py:105
  532.2 20.1 %collective-permute-start.68 = (bf16[2,256,256]{1,2,0:T(8,128)(2,1)S(1)}, bf16[2,256,256]{1,2,0:T(8,128)(2,1)S(1)}, u32[]{:S(2)}, u32[]{:S(2)}) collective-permute-start(bf16[2,256,256]{1,2,0:T(8,128)(2,1)S(1)} %get-tuple-element.187), channel_id=1, source_target_pairs={{0,16},{4,20},{8,24},{12,28},{16,0},{20,4},{24,8},{28,12},{1,17},{... | collective-permute-start | bytes 786440 | tf_op jit(solution)/shard_map/ppermute | solution.py:41
  535.4 17.9 %collective-permute-start.72 = (bf16[2,2,256,128]{2,3,0,1:T(8,128)(2,1)S(1)}, bf16[2,2,256,128]{2,3,0,1:T(8,128)(2,1)}, u32[]{:S(2)}, u32[]{:S(2)}) collective-permute-start(bf16[2,2,256,128]{2,3,0,1:T(8,128)(2,1)S(1)} %get-tuple-element.185), channel_id=1, source_target_pairs={{0,4},{4,0},{8,12},{12,8},{16,20},{20,16},{24,28},{28,24},{1,5},{5... | collective-permute-start | bytes 786440 | tf_op jit(solution)/shard_map/ppermute | solution.py:41
  553.3 56.5 %collective-permute-start.69 = (bf16[2,2,256,256]{2,3,1,0:T(8,128)(2,1)}, bf16[2,2,256,256]{2,3,1,0:T(8,128)(2,1)}, u32[]{:S(2)}, u32[]{:S(2)}) collective-permute-start(bf16[2,2,256,256]{2,3,1,0:T(8,128)(2,1)} %get-tuple-element.144), channel_id=1, source_target_pairs={{0,4},{4,0},{8,12},{12,8},{16,20},{20,16},{24,28},{28,24},{1,5},{5... | collective-permute-start | bytes 1572872 | tf_op jit(solution)/shard_map/ppermute | solution.py:41
  (162 other events, 2757.2 us)
Sparse Core Ops, SparseCore 0:
  550.0 53.3 all-reduce.10
